TPU v7x, 32 devices: a whole 2x2x4 slice. The times are simulated.
32 devices in a mesh: dp: 4 (over z), row: 4 (over x, core), col: 2 (over y).
Axes of the slice: x: 2, y: 2, z: 4, core: 2. Of those that a mesh axis runs over, the one named last changes fastest.
Arguments:
- inputs: float32 [768, 16384], P('row', ('dp', 'col')), may hold values from -6 to 6
- teacher: float32 [768, 16384], P('row', ('dp', 'col')), may hold values from -6 to 6
- lengths: int32 [8], P('dp'), may hold values from 1024 to 2048, as said below
- omega: bfloat16 [12, 64, 256], P('col'), may hold values from -4 to 4
- w_query: float32 [768, 768], P('row', 'col'), may hold values from -0.21875 to 0.21875
- b_query: float32 [768], P('col'), may hold values from -1.5 to 1.5
- w_key: float32 [768, 768], P('row', 'col'), may hold values from -0.21875 to 0.21875
- b_key: float32 [768], P('col'), may hold values from -1.5 to 1.5
- w_value: float32 [768, 768], P('row', 'col'), may hold values from -0.21875 to 0.21875
- b_value: float32 [768], P('col'), may hold values from -1.5 to 1.5
- w_out: float32 [768, 768], P('row', 'col'), may hold values from -0.875 to 0.875
- b_out: float32 [768], P('row'), may hold values from -1.5 to 1.5
- norm1_gain: float32 [768], P('row'), may hold values from 0.5 to 1.5
- norm1_bias: float32 [768], P('row'), may hold values from -1.5 to 1.5
- w_up: float32 [768, 3072], P('row', 'col'), may hold values from -0.21875 to 0.21875
- up_bias: float32 [3072], P('col'), may hold values from -1.5 to 1.5
- w_down: float32 [768, 3072], P('row', 'col'), may hold values from -0.109375 to 0.109375
- b_down: float32 [768], P('row'), may hold values from -1.5 to 1.5
- norm2_gain: float32 [768], P('row'), may hold values from 0.5 to 1.5
- norm2_bias: float32 [768], P('row'), may hold values from -1.5 to 1.5
Outputs:
- output: float32 [768, 16384], P('row', ('dp', 'col'))
- loss: float32 [], replicated
- grad_input: float32 [768, 16384], P('row', ('dp', 'col'))
- grad_w_query: float32 [768, 768], P('row', 'col')
- grad_b_query: float32 [768], P('col')
- grad_w_key: float32 [768, 768], P('row', 'col')
- grad_b_key: float32 [768], P('col')
- grad_w_value: float32 [768, 768], P('row', 'col')
- grad_b_value: float32 [768], P('col')
- grad_w_out: float32 [768, 768], P('row', 'col')
- grad_b_out: float32 [768], P('row')
- grad_norm1_gain: float32 [768], P('row')
- grad_norm1_bias: float32 [768], P('row')
- grad_w_up: float32 [768, 3072], P('row', 'col')
- grad_b_up: float32 [3072], P('col')
- grad_w_down: float32 [768, 3072], P('row', 'col')
- grad_b_down: float32 [768], P('row')
- grad_norm2_gain: float32 [768], P('row')
- grad_norm2_bias: float32 [768], P('row')
Inputs may be any that keep to these rules, and one draw needn't show every extreme that they name: `lengths`: every draw has a sequence with all 2048 tokens valid and one with 1024.
All inputs are finite; a program needn't handle non-finite values.
Results may differ from a plain program's by a relative error of at most 0.025.
Values may be sent and summed in bfloat16 or wider, within the bound.
No kernel may reach another device: no remote copies, remote signals or barrier semaphores. Data moves between devices by JAX's collectives and lax.ppermute only.
A program may use at most 256 MiB of HBM per device.

v0:
```python
import jax
import jax.numpy as jnp
from jax import lax
from jax.sharding import PartitionSpec as P

LOSS_SCALE = 16777216


stabilizer = 2.0
norm_eps = 1e-12
root_half = 0.7071067811865476
inv_root_two_pi = 0.3989422804014327


def seq_whole(segment):
    return lax.all_gather(segment, "col", axis=0, tiled=True)


def pos_whole(segment):
    return lax.all_gather(segment, "row", axis=0, tiled=True)


def seq_reduce(partial_term):
    return lax.psum_scatter(partial_term, "col", scatter_dimension=0, tiled=True)


def row_single(values):
    return lax.psum(values, "row")


def row_pair(first_term, second_term):
    return lax.psum((first_term, second_term), "row")


def positive_product(whole, weight, form):
    return lax.psum_scatter(
        jnp.einsum(form, whole, weight, preferred_element_type=jnp.float32),
        "row",
        scatter_dimension=0,
        tiled=True,
    )


def gelu_slope(values):
    return 0.5 * (1.0 + lax.erf(values * root_half)) + values * inv_root_two_pi * jnp.exp(
        -0.5 * values * values
    )


def positive(scaled, omega, keeper):
    exponent = jnp.einsum(
        "lshd,hdm->lshm", scaled.astype(jnp.bfloat16), omega, preferred_element_type=jnp.float32
    )
    return keeper * jnp.exp(
        exponent - 0.5 * jnp.sum(scaled * scaled, axis=-1, keepdims=True) - stabilizer
    )


def feature_back(grad_feat, feat, scaled, omega, factor):
    grad_expo = grad_feat * feat
    grad_scaled = jnp.einsum(
        "lshm,hdm->lshd", grad_expo.astype(jnp.bfloat16), omega, preferred_element_type=jnp.float32
    )
    grad_scaled = grad_scaled - jnp.sum(grad_expo, axis=-1, keepdims=True) * scaled
    return (factor * grad_scaled).astype(jnp.bfloat16)


def norm_forward(summed, gain, shift, width):
    average = row_single(jnp.sum(summed, axis=-1)) / width
    centered = summed - average[..., None]
    spread = row_single(jnp.sum(centered * centered, axis=-1)) / width
    scaling = lax.rsqrt(spread + norm_eps)
    normal = centered * scaling[..., None]
    return (normal * gain + shift, normal, scaling)


def norm_backward(grad_out, normal, scaling, gain, width):
    scaled_grad = grad_out * gain
    first_sum, second_sum = row_pair(
        jnp.sum(scaled_grad, axis=-1), jnp.sum(scaled_grad * normal, axis=-1)
    )
    grad_in = scaling[..., None] * (
        scaled_grad - first_sum[..., None] / width - normal * second_sum[..., None] / width
    )
    gain_grad = jnp.sum(grad_out * normal, axis=(0, 1))
    shift_grad = jnp.sum(grad_out, axis=(0, 1))
    return (grad_in, gain_grad, shift_grad)


def shards(
    inputs,
    teacher,
    lengths,
    omega,
    w_query,
    b_query,
    w_key,
    b_key,
    w_value,
    b_value,
    w_out,
    b_out,
    norm1_gain,
    norm1_bias,
    w_up,
    up_bias,
    w_down,
    b_down,
    norm2_gain,
    norm2_bias,
):
    row_parts = lax.axis_size("row")
    col_parts = lax.axis_size("col")
    seq_group = lengths.shape[0]
    seq_local = seq_group // col_parts
    seq_length = inputs.shape[1] // seq_local
    feat_local = inputs.shape[0]
    width = feat_local * row_parts
    head_local, head_width, feat_count = omega.shape
    pos_local = seq_length // row_parts
    head_block = head_local * head_width
    factor = head_width ** (-0.25)
    states = jnp.transpose(inputs).reshape(seq_local, seq_length, feat_local)
    target = jnp.transpose(teacher).reshape(seq_local, seq_length, feat_local)
    own_lengths = lax.dynamic_slice_in_dim(lengths, lax.axis_index("col") * seq_local, seq_local)
    keep_own = (jnp.arange(seq_length, dtype=jnp.int32)[None, :] < own_lengths[:, None]).astype(
        jnp.float32
    )
    positions = lax.axis_index("row") * pos_local + jnp.arange(pos_local, dtype=jnp.int32)
    keep_pos = (positions[:, None] < lengths[None, :]).astype(jnp.float32)
    states_low = states.astype(jnp.bfloat16)
    states_complete = seq_whole(states_low)
    triple_weight = jnp.concatenate((w_query, w_key, w_value), axis=1).astype(jnp.bfloat16)
    triple_bias = jnp.concatenate((b_query, b_key, b_value))
    output_weight_reduced = jnp.transpose(w_out).astype(jnp.bfloat16)
    triple_projection = (
        positive_product(states_complete, triple_weight, "zip,pc->izc") + triple_bias
    )
    triple_projection = triple_projection.reshape(pos_local, seq_group, 3, head_local, head_width)
    query_scaled = triple_projection[:, :, 0] * factor
    key_scaled = triple_projection[:, :, 1] * factor
    value_low = triple_projection[:, :, 2].astype(jnp.bfloat16)
    feat_query = positive(query_scaled, omega, 1.0)
    feat_key = positive(key_scaled, omega, keep_pos[:, :, None, None])
    query_low = feat_query.astype(jnp.bfloat16)
    key_low = feat_key.astype(jnp.bfloat16)
    kv_sum, key_total = row_pair(
        jnp.einsum("lshm,lshd->shmd", key_low, value_low, preferred_element_type=jnp.float32),
        jnp.sum(feat_key, axis=0),
    )
    kv_low = kv_sum.astype(jnp.bfloat16)
    total_low = key_total.astype(jnp.bfloat16)
    numerator = jnp.einsum("lshm,shmd->lshd", query_low, kv_low, preferred_element_type=jnp.float32)
    denominator = jnp.einsum(
        "lshm,shm->lsh", query_low, total_low, preferred_element_type=jnp.float32
    )
    attended = numerator / denominator[..., None]
    attended_low = attended.astype(jnp.bfloat16).reshape(pos_local, seq_group, head_block)
    attended_complete = pos_whole(attended_low)
    out_branch = (
        seq_reduce(
            jnp.einsum(
                "yvg,gu->vyu",
                attended_complete,
                output_weight_reduced,
                preferred_element_type=jnp.float32,
            )
        )
        + b_out
    )
    normed, normal_one, scale_one = norm_forward(states + out_branch, norm1_gain, norm1_bias, width)
    normed_low = normed.astype(jnp.bfloat16)
    normed_complete = seq_whole(normed_low)
    up_weight_reduced = w_up.astype(jnp.bfloat16)
    down_weight_reduced = jnp.transpose(w_down).astype(jnp.bfloat16)
    expanded_states = positive_product(normed_complete, up_weight_reduced, "zip,pc->izc") + up_bias
    hidden_low = jax.nn.gelu(expanded_states, approximate=False).astype(jnp.bfloat16)
    hidden_complete = pos_whole(hidden_low)
    down_branch = seq_reduce(
        jnp.einsum(
            "yvg,gu->vyu", hidden_complete, down_weight_reduced, preferred_element_type=jnp.float32
        )
    )
    down_branch = down_branch + b_down
    output, normal_two, scale_two = norm_forward(
        normed + down_branch, norm2_gain, norm2_bias, width
    )
    differ = output - target
    loss_part = jnp.sum(keep_own[..., None] * differ * differ)
    first_device = jnp.logical_and(lax.axis_index("row") == 0, lax.axis_index("col") == 0)
    count_part = jnp.where(first_device, jnp.sum(lengths).astype(jnp.float32), jnp.float32(0.0))
    loss_total, count = lax.psum((loss_part, count_part), ("dp", "row", "col"))
    loss = loss_total / (count * width)
    grad_output = 2.0 * LOSS_SCALE / (count * width) * keep_own[..., None] * differ
    grad_two, gain_two_grad, shift_two_grad = norm_backward(
        grad_output, normal_two, scale_two, norm2_gain, width
    )
    grad_down_low = grad_two.astype(jnp.bfloat16)
    down_gradient_complete = seq_whole(grad_down_low)
    b_down_grad = jnp.sum(down_gradient_complete, axis=(0, 1), dtype=jnp.float32)
    w_down_grad = jnp.einsum(
        "rku,krp->up", hidden_complete, down_gradient_complete, preferred_element_type=jnp.float32
    )
    hidden_gradient = positive_product(down_gradient_complete, down_weight_reduced, "gau,xu->agx")
    grad_up_low = (hidden_gradient * gelu_slope(expanded_states)).astype(jnp.bfloat16)
    up_gradient_complete = pos_whole(grad_up_low)
    b_up_grad = jnp.sum(up_gradient_complete, axis=(0, 1), dtype=jnp.float32)
    w_up_grad = jnp.einsum(
        "yrf,ryk->fk", normed_complete, up_gradient_complete, preferred_element_type=jnp.float32
    )
    grad_normed = seq_reduce(
        jnp.einsum(
            "cba,ua->bcu",
            up_gradient_complete,
            up_weight_reduced,
            preferred_element_type=jnp.float32,
        )
    )
    grad_one, gain_one_grad, shift_one_grad = norm_backward(
        grad_two + grad_normed, normal_one, scale_one, norm1_gain, width
    )
    grad_attn_low = grad_one.astype(jnp.bfloat16)
    attention_gradient_complete = seq_whole(grad_attn_low)
    b_out_grad = jnp.sum(attention_gradient_complete, axis=(0, 1), dtype=jnp.float32)
    w_out_grad = jnp.einsum(
        "rku,krp->up",
        attended_complete,
        attention_gradient_complete,
        preferred_element_type=jnp.float32,
    )
    attended_gradient = positive_product(
        attention_gradient_complete, output_weight_reduced, "gau,xu->agx"
    )
    attended_gradient = attended_gradient.reshape(pos_local, seq_group, head_local, head_width)
    grad_numer = (attended_gradient / denominator[..., None]).astype(jnp.bfloat16)
    grad_denom = (-jnp.sum(attended_gradient * attended, axis=-1) / denominator).astype(
        jnp.bfloat16
    )
    grad_kv, grad_total = row_pair(
        jnp.einsum("lshm,lshd->shmd", query_low, grad_numer, preferred_element_type=jnp.float32),
        jnp.einsum("lshm,lsh->shm", query_low, grad_denom, preferred_element_type=jnp.float32),
    )
    grad_kv_low = grad_kv.astype(jnp.bfloat16)
    grad_feat_query = jnp.einsum(
        "lshd,shmd->lshm", grad_numer, kv_low, preferred_element_type=jnp.float32
    )
    grad_feat_query = grad_feat_query + grad_denom.astype(jnp.float32)[
        ..., None
    ] * total_low.astype(jnp.float32)
    grad_query = feature_back(grad_feat_query, feat_query, query_scaled, omega, factor)
    grad_feat_key = jnp.einsum(
        "lshd,shmd->lshm", value_low, grad_kv_low, preferred_element_type=jnp.float32
    )
    grad_feat_key = grad_feat_key + grad_total
    grad_key = feature_back(grad_feat_key, feat_key, key_scaled, omega, factor)
    grad_value = jnp.einsum(
        "lshm,shmd->lshd", key_low, grad_kv_low, preferred_element_type=jnp.float32
    ).astype(jnp.bfloat16)
    grad_triple = jnp.stack((grad_query, grad_key, grad_value), axis=2).reshape(
        pos_local, seq_group, 3 * head_block
    )
    triple_gradient_complete = pos_whole(grad_triple)
    b_triple_grad = jnp.sum(triple_gradient_complete, axis=(0, 1), dtype=jnp.float32)
    w_triple_grad = jnp.einsum(
        "yrf,ryk->fk", states_complete, triple_gradient_complete, preferred_element_type=jnp.float32
    )
    grad_input = grad_one + seq_reduce(
        jnp.einsum(
            "cba,ua->bcu",
            triple_gradient_complete,
            triple_weight,
            preferred_element_type=jnp.float32,
        )
    )
    (
        w_triple_grad,
        b_triple_grad,
        w_out_grad,
        b_out_grad,
        w_up_grad,
        b_up_grad,
        w_down_grad,
        b_down_grad,
    ) = (
        lax.psum(w_triple_grad.astype(jnp.bfloat16), "dp").astype(jnp.float32),
        lax.psum(b_triple_grad.astype(jnp.bfloat16), "dp").astype(jnp.float32),
        lax.psum(w_out_grad.astype(jnp.bfloat16), "dp").astype(jnp.float32),
        lax.psum(b_out_grad.astype(jnp.bfloat16), "dp").astype(jnp.float32),
        lax.psum(w_up_grad.astype(jnp.bfloat16), "dp").astype(jnp.float32),
        lax.psum(b_up_grad.astype(jnp.bfloat16), "dp").astype(jnp.float32),
        lax.psum(w_down_grad.astype(jnp.bfloat16), "dp").astype(jnp.float32),
        lax.psum(b_down_grad.astype(jnp.bfloat16), "dp").astype(jnp.float32),
    )
    gain_one_grad, shift_one_grad, gain_two_grad, shift_two_grad = lax.psum(
        (gain_one_grad, shift_one_grad, gain_two_grad, shift_two_grad), ("dp", "col")
    )
    token_rows = seq_local * seq_length
    return (
        jnp.transpose(output.reshape(token_rows, feat_local)),
        loss,
        jnp.transpose(grad_input.reshape(token_rows, feat_local)),
        w_triple_grad[:, :head_block],
        b_triple_grad[:head_block],
        w_triple_grad[:, head_block : 2 * head_block],
        b_triple_grad[head_block : 2 * head_block],
        w_triple_grad[:, 2 * head_block :],
        b_triple_grad[2 * head_block :],
        jnp.transpose(w_out_grad),
        b_out_grad,
        gain_one_grad,
        shift_one_grad,
        w_up_grad,
        b_up_grad,
        jnp.transpose(w_down_grad),
        b_down_grad,
        gain_two_grad,
        shift_two_grad,
    )


def solution(mesh):
    in_specs = (
        P("row", ("dp", "col")),
        P("row", ("dp", "col")),
        P("dp"),
        P("col", None, None),
        P("row", "col"),
        P("col"),
        P("row", "col"),
        P("col"),
        P("row", "col"),
        P("col"),
        P("row", "col"),
        P("row"),
        P("row"),
        P("row"),
        P("row", "col"),
        P("col"),
        P("row", "col"),
        P("row"),
        P("row"),
        P("row"),
    )
    out_specs = (
        P("row", ("dp", "col")),
        P(),
        P("row", ("dp", "col")),
        P("row", "col"),
        P("col"),
        P("row", "col"),
        P("col"),
        P("row", "col"),
        P("col"),
        P("row", "col"),
        P("row"),
        P("row"),
        P("row"),
        P("row", "col"),
        P("col"),
        P("row", "col"),
        P("row"),
        P("row"),
        P("row"),
    )
    return jax.shard_map(shards, mesh=mesh, in_specs=in_specs, out_specs=out_specs, check_vma=False)
```

profile of v0, /device:TPU:0, one launch (start us, length us, event | category | flops | bytes accessed | tf_op | source)
XLA Modules:
  0.0 1462.0 jit_solution(4006246865171864660)
XLA Ops:
  10.0 30.1 %all-gather.24.cloned.1.call-done = bf16[4096,192]{0,1:T(8,128)(2,1)} async-done(((bf16[2048,192]{0,1:T(8,128)(2,1)}), bf16[4096,192]{0,1:T(8,128)(2,1)}) %all-gather.24.cloned.1.call-update) | async-done | bytes 1572880 | tf_op jit(solution)/shard_map/all_gather | solution.py:16
  40.1 10.5 convolution_bitcast_fusion.2
  51.5 137.1 %reduce-scatter.9.cloned.1.call-done = f32[512,2,1152]{0,2,1:T(8,128)} async-done(((f32[2048,2,1152]{0,2,1:T(8,128)}), f32[512,2,1152]{0,2,1:T(8,128)}) %reduce-scatter.9.cloned.1.call-update) | async-done | bytes 4718608 | tf_op jit(solution)/shard_map/reduce_scatter | solution.py:36
  192.2 4.8 fusion.21
  197.1 4.1 fusion.22
  203.5 19.0 %all-reduce.12 = (bf16[2,6,256,64]{2,3,1,0:T(8,128)(2,1)S(1)}, bf16[2,6,256]{2,0,1:T(2,128)(2,1)S(1)}) all-reduce(f32[2,6,256,64]{2,3,1,0:T(8,128)S(1)} %fusion.24, f32[2,6,256]{2,0,1:T(2,128)S(1)} %get-tuple-element.54), channel_id=1, replica_groups=mesh['dp'=4,'row'=4,'col'=2] {'row'}, use_global_device_ids=true, to_apply=%region_2.0 | all-reduce | flops 199680 | bytes 1198080 | tf_op jit(solution)/shard_map/psum | solution.py:32
  229.6 29.2 %all-gather.10.cloned.1.call-done = bf16[2048,2,384]{2,0,1:T(8,128)(2,1)} async-done(((bf16[512,2,384]{2,0,1:T(8,128)(2,1)}), bf16[2048,2,384]{2,0,1:T(8,128)(2,1)}) %all-gather.10.cloned.1.call-update) | async-done | bytes 3145744 | tf_op jit(solution)/shard_map/all_gather | solution.py:20
  258.8 4.7 convolution_bitcast_fusion.7
  263.6 43.5 %reduce-scatter.11.cloned.1.call-done = f32[1,2048,192]{1,2,0:T(8,128)} async-done(((f32[2,2048,192]{1,2,0:T(8,128)}), f32[1,2048,192]{1,2,0:T(8,128)}) %reduce-scatter.11.cloned.1.call-update) | async-done | bytes 1572880 | tf_op jit(solution)/shard_map/reduce_scatter | solution.py:24
  308.8 6.5 psum.184
  315.6 6.1 psum.185
  323.5 26.2 %all-gather.12.cloned.1.call-done = bf16[2,2048,192]{1,2,0:T(8,128)(2,1)} async-done(((bf16[1,2048,192]{1,2,0:T(8,128)(2,1)}), bf16[2,2048,192]{1,2,0:T(8,128)(2,1)}) %all-gather.12.cloned.1.call-update) | async-done | bytes 1572880 | tf_op jit(solution)/shard_map/all_gather | solution.py:16
  349.7 11.6 convolution_bitcast_fusion.1
  361.4 182.0 %reduce-scatter.13.cloned.1.call-done = f32[512,2,1536]{2,0,1:T(8,128)} async-done(((f32[2048,2,1536]{2,0,1:T(8,128)}), f32[512,2,1536]{2,0,1:T(8,128)}) %reduce-scatter.13.cloned.1.call-update) | async-done | bytes 6291472 | tf_op jit(solution)/shard_map/reduce_scatter | solution.py:36
  543.4 15.9 %fusion.2 = bf16[512,2,1536]{2,0,1:T(8,128)(2,1)} fusion(f32[512,2,1536]{2,0,1:T(8,128)} %reduce-scatter.13.cloned.1.call-done, f32[1536]{0:T(1024)S(1)} %copy-done.36), kind=kLoop, calls=%fused_computation.7 | loop fusion | flops 103809024 | bytes 9443328 | tf_op jit(solution)/shard_map/convert_element_type | solution.py:177
  559.4 82.2 %all-gather.14.cloned.1.call-done = bf16[2048,2,1536]{2,0,1:T(8,128)(2,1)} async-done(((bf16[512,2,1536]{2,0,1:T(8,128)(2,1)}), bf16[2048,2,1536]{2,0,1:T(8,128)(2,1)}) %all-gather.14.cloned.1.call-update) | async-done | bytes 12582928 | tf_op jit(solution)/shard_map/all_gather | solution.py:20
  641.6 10.5 convolution_bitcast_fusion.6
  653.4 40.3 %psum.189 = f32[]{:T(128)} all-reduce(f32[]{:T(128)S(6)} %select_n.8), channel_id=1, replica_groups=mesh['dp'=4,'row'=4,'col'=2] {'dp','row','col'}, use_global_device_ids=true, to_apply=%region_20.21 | all-reduce | flops 1 | bytes 8 | tf_op jit(solution)/shard_map/psum | solution.py:192
  698.9 6.9 psum.186
  706.0 6.8 psum.187
  713.6 4.8 multiply_reduce_fusion
  718.4 11.6 all-reduce.3
  734.4 26.4 %all-gather.16.cloned.1.call-done = bf16[2,2048,192]{1,2,0:T(8,128)(2,1)} async-done(((bf16[1,2048,192]{1,2,0:T(8,128)(2,1)}), bf16[2,2048,192]{1,2,0:T(8,128)(2,1)}) %all-gather.16.cloned.1.call-update) | async-done | bytes 1572880 | tf_op jit(solution)/shard_map/all_gather | solution.py:16
  760.9 13.5 convolution_bitcast_fusion
  774.5 182.0 %reduce-scatter.17.cloned.1.call-done = f32[512,2,1536]{2,0,1:T(8,128)} async-done(((f32[2048,2,1536]{2,0,1:T(8,128)}), f32[512,2,1536]{2,0,1:T(8,128)}) %reduce-scatter.17.cloned.1.call-update) | async-done | bytes 6291472 | tf_op jit(solution)/shard_map/reduce_scatter | solution.py:36
  956.5 8.2 fusion.7
  964.8 82.2 %all-gather.18.cloned.1.call-done = bf16[2048,2,1536]{2,0,1:T(8,128)(2,1)} async-done(((bf16[512,2,1536]{2,0,1:T(8,128)(2,1)}), bf16[2048,2,1536]{2,0,1:T(8,128)(2,1)}) %all-gather.18.cloned.1.call-update) | async-done | bytes 12582928 | tf_op jit(solution)/shard_map/all_gather | solution.py:20
  1047.0 10.7 convolution_bitcast_fusion.5
  1057.8 43.5 %reduce-scatter.19.cloned.1.call-done = f32[1,2048,192]{1,2,0:T(8,128)} async-done(((f32[2,2048,192]{1,2,0:T(8,128)}), f32[1,2048,192]{1,2,0:T(8,128)}) %reduce-scatter.19.cloned.1.call-update) | async-done | bytes 1572880 | tf_op jit(solution)/shard_map/reduce_scatter | solution.py:24
  1101.3 4.9 multiply_reduce_fusion.1
  1106.3 11.4 all-reduce.2
  1120.5 26.8 %all-gather.20.cloned.1.call-done = bf16[2,2048,192]{1,2,0:T(8,128)(2,1)} async-done(((bf16[1,2048,192]{1,2,0:T(8,128)(2,1)}), bf16[2,2048,192]{1,2,0:T(8,128)(2,1)}) %all-gather.20.cloned.1.call-update) | async-done | bytes 1572880 | tf_op jit(solution)/shard_map/all_gather | solution.py:16
  1147.4 5.3 convolution_bitcast_fusion.3
  1154.0 57.7 %reduce-scatter.21.cloned.1.call-done = f32[512,2,384]{2,0,1:T(8,128)} async-done(((f32[2048,2,384]{2,0,1:T(8,128)}), f32[512,2,384]{2,0,1:T(8,128)}) %reduce-scatter.21.cloned.1.call-update) | async-done | bytes 1572880 | tf_op jit(solution)/shard_map/reduce_scatter | solution.py:36
  1217.2 19.0 %all-reduce.13 = (bf16[2,6,256,64]{2,3,1,0:T(8,128)(2,1)S(1)}, f32[2,6,256]{2,0,1:T(2,128)S(1)}) all-reduce(f32[2,6,256,64]{2,3,1,0:T(8,128)S(1)} %fusion.35, f32[2,6,256]{2,0,1:T(2,128)S(1)} %bitcast.280), channel_id=1, replica_groups=mesh['dp'=4,'row'=4,'col'=2] {'row'}, use_global_device_ids=true, to_apply=%region_34.35 | all-reduce | flops 199680 | bytes 1204224 | tf_op jit(solution)/shard_map/psum | solution.py:32
  1239.4 5.1 fusion.119
  1252.7 4.3 copy.89
  1258.5 8.1 fusion.33
  1266.6 10.0 fusion.30
  1278.3 43.7 %all-gather.22.cloned.1.call-done = bf16[2048,2,1152]{2,0,1:T(8,128)(2,1)} async-done(((bf16[512,2,1152]{2,0,1:T(8,128)(2,1)}), bf16[2048,2,1152]{2,0,1:T(8,128)(2,1)}) %all-gather.22.cloned.1.call-update) | async-done | bytes 9437200 | tf_op jit(solution)/shard_map/all_gather | solution.py:20
  1322.1 7.1 fusion.34
  1329.3 8.8 convolution_bitcast_fusion.4
  1338.1 41.4 %psum.188 = f32[]{:T(128)} all-reduce(f32[]{:T(128)} %get-tuple-element.26), channel_id=1, replica_groups=mesh['dp'=4,'row'=4,'col'=2] {'dp','row','col'}, use_global_device_ids=true, to_apply=%region_18.0 | all-reduce | flops 1 | bytes 8 | tf_op jit(solution)/shard_map/psum | solution.py:192
  1381.9 6.4 reduce_sum.272
  1388.4 22.3 %all-reduce = (f32[192]{0:T(256)}, f32[192]{0:T(256)}, f32[192]{0:T(256)}, f32[192]{0:T(256)}) all-reduce(f32[192]{0:T(256)S(1)} %copy-done.45, f32[192]{0:T(256)S(1)} %copy-done.46, f32[192]{0:T(256)S(1)} %copy-done.43, f32[192]{0:T(256)S(1)} %copy-done.44), channel_id=1, replica_groups=mesh['dp'=4,'row'=4,'col'=2] {'dp','col'}, use_global_device_ids=true, to_apply=%region_45.46 | all-reduce | flops 768 | bytes 6144 | tf_op jit(solution)/shard_map/psum | solution.py:294
  1411.0 6.0 reduce_sum.268
  1417.0 8.7 all-reduce.5
  1434.2 16.6 %reduce-scatter.23.cloned.1.call-done = f32[1,2048,192]{1,2,0:T(8,128)} async-done(((f32[2,2048,192]{1,2,0:T(8,128)}), f32[1,2048,192]{1,2,0:T(8,128)}) %reduce-scatter.23.cloned.1.call-update) | async-done | bytes 1572880 | tf_op jit(solution)/shard_map/reduce_scatter | solution.py:24
  (212 shorter events, 68.5 us)
Async XLA Ops:
  7.2 185.0 %copy-start = (bf16[6,64,256]{2,1,0:T(8,128)(2,1)S(1)}, bf16[6,64,256]{2,1,0:T(8,128)(2,1)}, u32[]{:S(2)}) copy-start(bf16[6,64,256]{2,1,0:T(8,128)(2,1)} %param.23) | copy-start | bytes 589828
  7.2 32.9 %all-gather.24.cloned.1.call-start = ((), (), s32[]{:S(2)}) async-start(), calls=%async_computation.23 | async-start | bytes 2359296 | tf_op jit(solution)/shard_map/all_gather | solution.py:16
  9.8 178.7 %reduce-scatter.9.cloned.1.call-start = ((), (), s32[]{:S(2)}) async-start(), calls=%async_computation.8 | async-start | bytes 23592960 | tf_op jit(solution)/shard_map/reduce_scatter | solution.py:36
  9.9 40.7 %copy-start.18 = (bf16[192,384]{1,0:T(8,128)(2,1)}, bf16[192,384]{1,0:T(8,128)(2,1)S(1)}, u32[]{:S(2)}) copy-start(bf16[192,384]{1,0:T(8,128)(2,1)S(1)} %convert.19) | copy-start | bytes 442372
  10.0 40.7 %copy-start.19 = (bf16[192,384]{1,0:T(8,128)(2,1)}, bf16[192,384]{1,0:T(8,128)(2,1)S(1)}, u32[]{:S(2)}) copy-start(bf16[192,384]{1,0:T(8,128)(2,1)S(1)} %convert.20) | copy-start | bytes 442372
  50.7 208.1 %all-gather.10.cloned.1.call-start = ((), (), s32[]{:S(2)}) async-start(), calls=%async_computation.9 | async-start | bytes 3932160 | tf_op jit(solution)/shard_map/all_gather | solution.py:20
  51.5 145.6 %copy-start.39 = (f32[512,2]{0,1:T(2,128)}, f32[512,2]{0,1:T(2,128)S(1)}, u32[]{:S(2)}) copy-start(f32[512,2]{0,1:T(2,128)S(1)} %compare_convert_fusion) | copy-start | bytes 12292
  191.2 9.9 copy-start.8
  191.6 5.4 copy-start.4
  191.6 5.4 copy-start.6
  222.5 5.9 copy-start.34
  222.5 5.9 copy-start.52
  228.4 30.4 %copy-start.20 = (f32[192,384]{1,0:T(8,128)S(1)}, f32[192,384]{1,0:T(8,128)}, u32[]{:S(2)}) copy-start(f32[192,384]{1,0:T(8,128)} %param.30) | copy-start | bytes 884740
  229.6 77.6 %reduce-scatter.11.cloned.1.call-start = ((), (), s32[]{:S(2)}) async-start(), calls=%async_computation.10 | async-start | bytes 4718592 | tf_op jit(solution)/shard_map/reduce_scatter | solution.py:24
  263.5 43.6 %copy-start.10 = (f32[192,2048]{1,0:T(8,128)S(1)}, f32[192,2048]{1,0:T(8,128)}, u32[]{:S(2)}) copy-start(f32[192,2048]{1,0:T(8,128)} %param.20) | copy-start | bytes 4718596
  263.5 43.6 %copy-start.50 = (f32[192]{0:T(256)S(1)}, f32[192]{0:T(256)}, u32[]{:S(2)}) copy-start(f32[192]{0:T(256)} %param.31) | copy-start | bytes 2308
  263.6 58.1 %copy-start.37 = (f32[192]{0:T(256)S(1)}, f32[192]{0:T(256)}, u32[]{:S(2)}) copy-start(f32[192]{0:T(256)} %param.32) | copy-start | bytes 2308
  263.6 58.1 %copy-start.42 = (f32[192]{0:T(256)S(1)}, f32[192]{0:T(256)}, u32[]{:S(2)}) copy-start(f32[192]{0:T(256)} %param.33) | copy-start | bytes 2308
  263.6 86.1 %all-gather.12.cloned.1.call-start = ((), (), s32[]{:S(2)}) async-start(), calls=%async_computation.11 | async-start | bytes 2359296 | tf_op jit(solution)/shard_map/all_gather | solution.py:16
  315.4 34.3 %copy-start.23 = (f32[192,1536]{1,0:T(8,128)S(1)}, f32[192,1536]{1,0:T(8,128)}, u32[]{:S(2)}) copy-start(f32[192,1536]{1,0:T(8,128)} %param.34) | copy-start | bytes 3538948
  322.9 220.5 %reduce-scatter.13.cloned.1.call-start = ((), (), s32[]{:S(2)}) async-start(), calls=%async_computation.12 | async-start | bytes 31457280 | tf_op jit(solution)/shard_map/reduce_scatter | solution.py:36
  361.4 182.1 %copy-start.36 = (f32[1536]{0:T(1024)S(1)}, f32[1536]{0:T(1024)}, u32[]{:S(2)}) copy-start(f32[1536]{0:T(1024)} %param.35) | copy-start | bytes 18436
  361.4 280.2 %all-gather.14.cloned.1.call-start = ((), (), s32[]{:S(2)}) async-start(), calls=%async_computation.13 | async-start | bytes 15728640 | tf_op jit(solution)/shard_map/all_gather | solution.py:20
  559.3 82.3 %copy-start.22 = (f32[192,1536]{1,0:T(8,128)S(1)}, f32[192,1536]{1,0:T(8,128)}, u32[]{:S(2)}) copy-start(f32[192,1536]{1,0:T(8,128)} %param.36) | copy-start | bytes 3538948
  559.3 137.7 %reduce-scatter.15.cloned.1.call-start = ((), (), s32[]{:S(2)}) async-start(), calls=%async_computation.14 | async-start | bytes 4718592 | tf_op jit(solution)/shard_map/reduce_scatter | solution.py:24
  652.1 108.8 %all-gather.16.cloned.1.call-start = ((), (), s32[]{:S(2)}) async-start(), calls=%async_computation.15 | async-start | bytes 2359296 | tf_op jit(solution)/shard_map/all_gather | solution.py:16
  734.2 222.3 %reduce-scatter.17.cloned.1.call-start = ((), (), s32[]{:S(2)}) async-start(), calls=%async_computation.16 | async-start | bytes 31457280 | tf_op jit(solution)/shard_map/reduce_scatter | solution.py:36
  774.4 272.6 %all-gather.18.cloned.1.call-start = ((), (), s32[]{:S(2)}) async-start(), calls=%async_computation.17 | async-start | bytes 15728640 | tf_op jit(solution)/shard_map/all_gather | solution.py:20
  964.7 136.6 %reduce-scatter.19.cloned.1.call-start = ((), (), s32[]{:S(2)}) async-start(), calls=%async_computation.18 | async-start | bytes 4718592 | tf_op jit(solution)/shard_map/reduce_scatter | solution.py:24
  1057.7 89.6 %all-gather.20.cloned.1.call-start = ((), (), s32[]{:S(2)}) async-start(), calls=%async_computation.19 | async-start | bytes 2359296 | tf_op jit(solution)/shard_map/all_gather | solution.py:16
  1117.6 29.7 %copy-start.21 = (f32[192,384]{1,0:T(8,128)S(1)}, f32[192,384]{1,0:T(8,128)}, u32[]{:S(2)}) copy-start(f32[192,384]{1,0:T(8,128)} %param.30) | copy-start | bytes 884740
  1120.5 91.2 %reduce-scatter.21.cloned.1.call-start = ((), (), s32[]{:S(2)}) async-start(), calls=%async_computation.20 | async-start | bytes 7864320 | tf_op jit(solution)/shard_map/reduce_scatter | solution.py:36
  1152.7 169.4 %all-gather.22.cloned.1.call-start = ((), (), s32[]{:S(2)}) async-start(), calls=%async_computation.21 | async-start | bytes 11796480 | tf_op jit(solution)/shard_map/all_gather | solution.py:20
  1236.2 8.3 slice-start
  1239.4 5.2 slice-start.1
  1239.4 5.2 copy-start.15
  1257.1 170.9 %all-reduce.11.cloned.1.call-start = ((), (), s32[]{:S(2)}) async-start(), calls=%async_computation.24 | async-start | bytes 3538944 | tf_op jit(solution)/shard_map/psum | solution.py:285
  1258.5 8.1 copy-start.17
  1266.6 10.0 copy-start.11
  1266.6 10.0 copy-start.13
  1329.2 121.5 %reduce-scatter.23.cloned.1.call-start = ((), (), s32[]{:S(2)}) async-start(), calls=%async_computation.22 | async-start | bytes 4718592 | tf_op jit(solution)/shard_map/reduce_scatter | solution.py:24
  1381.9 6.4 copy-start.43
  1381.9 6.4 copy-start.44
  1381.9 6.4 copy-start.45
  1381.9 6.4 copy-start.46
  1428.0 5.2 copy-start.16
  1429.8 21.0 %copy-start.9 = (f32[1,2048,192]{1,2,0:T(8,128)S(1)}, f32[1,2048,192]{1,2,0:T(8,128)}, u32[]{:S(2)}) copy-start(f32[1,2048,192]{1,2,0:T(8,128)} %get-tuple-element.48) | copy-start | bytes 4718596
  1429.8 21.0 %copy-start.38 = (f32[192]{0:T(256)S(1)}, f32[192]{0:T(256)}, u32[]{:S(2)}) copy-start(f32[192]{0:T(256)} %param.32) | copy-start | bytes 2308
  (25 other events, 64.5 us)
Sparse Core Ops, SparseCore 0:
  10.2 29.8 all-gather.23
  50.8 137.6 reduce-scatter.8
  229.7 29.0 all-gather.9
  263.7 43.4 reduce-scatter.10
  323.1 26.6 all-gather.11
  361.5 181.8 reduce-scatter.12
  559.4 82.0 all-gather.13
  652.2 44.8 reduce-scatter.14
  734.3 26.4 all-gather.15
  774.5 181.8 reduce-scatter.16
  964.9 82.0 all-gather.17
  1057.8 43.4 reduce-scatter.18
  1120.6 26.7 all-gather.19
  1152.8 58.8 reduce-scatter.20
  1257.2 64.7 all-gather.21
  1329.3 76.7 all-reduce.10
  1408.3 42.4 reduce-scatter.22
where the time goes:
time: 1470 us; the launch traced here: 1460 us
  waiting for transfers between devices  1010 us (69%)
  blocking collectives  200 us (14%)
  matrix products  133 us (9%)
  other arithmetic  81.9 us (6%)
  between operations  18.5 us (1%)
  local copies, waits for them, and re-layouts  17.2 us (1%)
    reduce_scatter x4, waiting for transfers between devices, positive_product(): lax.psum_scatter(jnp.einsum(form, whole, weight, preferred_element_type=j...  559 us
    all_gather x4, waiting for transfers between devices, pos_whole(): return lax.all_gather(segment, 'row', axis=0, tiled=True)  237 us
    all_gather x4, waiting for transfers between devices, seq_whole(): return lax.all_gather(segment, 'col', axis=0, tiled=True)  110 us
    reduce_scatter x4, waiting for transfers between devices, seq_reduce(): lax.psum_scatter(partial_term, 'col', scatter_dimension=0, tiled=True)  104 us
    psum x2, blocking collectives, shards(): loss_total, count = lax.psum((loss_part, count_part), ('dp', 'row', 'col'))  81.8 us
    psum x4, blocking collectives, row_pair(): return lax.psum((first_term, second_term), 'row')  61 us
    dot_general x4, matrix products, positive_product(): jnp.einsum(form, whole, weight, preferred_element_type=jnp.float32)  41 us
  transfers between devices with their start and end apart: 17, of which 16 were waited for; matrix products, arithmetic and copies ran while one was open for 4% of the time, Pallas kernels for 0%

commit v1 on v0

v1 whole, which is shorter than its diff:
```python
import jax
import jax.numpy as jnp
from jax import lax
from jax.sharding import PartitionSpec as P

LOSS_SCALE = 16777216

stabilizer = 2.0
norm_eps = 1e-12
root_half = 0.7071067811865476
inv_root_two_pi = 0.3989422804014327
f32 = jnp.float32
bf16 = jnp.bfloat16


def swap(value, axis, mask):
    size = lax.axis_size(axis)
    return lax.ppermute(value, axis, [(s, s ^ mask) for s in range(size)])


def dot(a, b, dims):
    return lax.dot_general(a, b, (dims, ((), ())), preferred_element_type=f32)


def gather_plane(own, share):
    cut = own.shape[0] * share // 4
    by_core = swap(own, "row", 1)
    by_x = swap(own, "row", 2)
    by_y = swap(own, "col", 1)
    far_x = swap(by_y[:cut], "row", 2)
    far_y = swap(by_x[cut:], "col", 1)
    far = jnp.concatenate((far_x, far_y), axis=0)
    x_core = swap(by_x, "row", 1)
    y_core = swap(by_y, "row", 1)
    far_core = swap(far, "row", 1)
    return ((own, by_core, by_x, x_core), (by_y, y_core, far, far_core))


def rows_of(blocks):
    return jnp.concatenate(blocks, axis=0)


def reduce_plane(mine, theirs, share):
    got = swap(jnp.stack(theirs).astype(bf16), "row", 1)
    near = mine[0] + got[0]
    far = mine[1] + got[1]
    cut = near.shape[0] * share // 4
    far_low = far[:, 1].astype(bf16)
    from_x = swap(far_low[:cut], "row", 2)
    from_y = swap(far_low[cut:], "col", 1)
    to_x = far[:, 0]
    to_y = near[:, 1]
    to_y = jnp.concatenate((to_y[:cut] + from_x, to_y[cut:]), axis=0).astype(bf16)
    to_x = jnp.concatenate((to_x[:cut], to_x[cut:] + from_y), axis=0).astype(bf16)
    from_x = swap(to_x, "row", 2)
    from_y = swap(to_y, "col", 1)
    return near[:, 0] + from_x + from_y


def reduce_dp(value):
    parts = lax.axis_size("dp")
    if parts != 4:
        return lax.psum(value.astype(bf16), "dp").astype(f32)
    index = lax.axis_index("dp")
    n = value.shape[0] // parts
    low = value.astype(bf16).reshape(parts, n, value.shape[1])
    total = lax.dynamic_index_in_dim(value.reshape(low.shape), index, 0, False)
    for mask in (1, 2, 3):
        total = total + swap(lax.dynamic_index_in_dim(low, index ^ mask, 0, False), "dp", mask)
    total = total.astype(bf16)
    out = jnp.zeros(low.shape, bf16)
    out = lax.dynamic_update_index_in_dim(out, total, index, 0)
    for mask in (1, 2, 3):
        out = lax.dynamic_update_index_in_dim(out, swap(total, "dp", mask), index ^ mask, 0)
    return out.reshape(value.shape).astype(f32)


def reduce_small(value, axes):
    for axis in axes:
        step = 1
        while step < lax.axis_size(axis):
            value = value + swap(value, axis, step)
            step *= 2
    return value


def to_positions(shard, row_parts):
    row = lax.axis_index("row")
    n = shard.shape[1] // row_parts
    blocks = []
    for j in range(row_parts):
        block = lax.dynamic_slice_in_dim(shard, (row ^ j) * n, n, 1).astype(bf16)
        blocks.append(swap(block, "row", j) if j else block)
    return jnp.concatenate(blocks, axis=0)


def to_features(value, row_parts):
    row = lax.axis_index("row")
    k = value.shape[0] // row_parts
    n = value.shape[1]
    out = jnp.zeros((k, n * row_parts), f32)
    for j in range(row_parts):
        block = value[j * k : (j + 1) * k]
        if j:
            block = swap(block.astype(bf16), "row", j).astype(f32)
        out = lax.dynamic_update_slice_in_dim(out, block, (row ^ j) * n, 1)
    return out


def row_vectors(packed):
    return jnp.concatenate([packed] + [swap(packed, "row", j) for j in (1, 2, 3)], axis=1)


def norm_forward(summed, gain, shift):
    average = jnp.mean(summed, axis=0, keepdims=True)
    centered = summed - average
    spread = jnp.mean(centered * centered, axis=0, keepdims=True)
    scaling = lax.rsqrt(spread + norm_eps)
    normal = centered * scaling
    return normal * gain[:, None] + shift[:, None], normal, scaling


def norm_backward(grad_out, normal, scaling, gain):
    scaled_grad = grad_out * gain[:, None]
    first = jnp.mean(scaled_grad, axis=0, keepdims=True)
    second = jnp.mean(scaled_grad * normal, axis=0, keepdims=True)
    grad_in = scaling * (scaled_grad - first - normal * second)
    return grad_in, jnp.sum(grad_out * normal, axis=1), jnp.sum(grad_out, axis=1)


def weight_grad(left, right, row_parts, share):
    n = left.shape[0] // row_parts
    cols, k, _ = right.shape
    flat = right.reshape(cols * k, -1)
    parts = [
        dot(left[j * n : (j + 1) * n], flat, ((1,), (1,))).reshape(n, cols, k)
        for j in range(row_parts)
    ]
    return reduce_dp(reduce_plane(parts[0::2], parts[1::2], share))


def shards(
    inputs, teacher, lengths, omega,
    w_query, b_query, w_key, b_key, w_value, b_value, w_out, b_out,
    norm1_gain, norm1_bias, w_up, up_bias, w_down, b_down, norm2_gain, norm2_bias,
):
    row_parts = lax.axis_size("row")
    cols = lax.axis_size("col")
    feat_local, seq_length = inputs.shape
    width = feat_local * row_parts
    head_local, head_width, feats = omega.shape
    heads = head_local * cols
    tokens = seq_length // row_parts
    head_block = head_local * head_width
    factor = head_width ** (-0.25)
    row = lax.axis_index("row")
    col = lax.axis_index("col")
    share = 1

    own_triple = jnp.concatenate((w_query, w_key, w_value), axis=1).astype(bf16)
    states = to_positions(inputs, row_parts)
    triple_blocks = gather_plane(own_triple, share)
    omega_all = jnp.concatenate((omega, swap(omega, "col", 1)), axis=0)
    col_pack = jnp.concatenate((b_query, b_key, b_value, up_bias))
    col_other = swap(col_pack, "col", 1)
    row_pack = row_vectors(jnp.stack((b_out, norm1_gain, norm1_bias, b_down, norm2_gain, norm2_bias)))
    b_out_all, gain1, shift1, b_down_all, gain2, shift2 = [row_pack[m] for m in range(6)]
    triple_bias = jnp.stack((col_pack[: 3 * head_block], col_other[: 3 * head_block]))
    up_bias_all = jnp.concatenate((col_pack[3 * head_block :], col_other[3 * head_block :]))
    out_blocks = gather_plane(w_out.astype(bf16), share)
    up_blocks = gather_plane(w_up.astype(bf16), share)
    down_blocks = gather_plane(w_down.astype(bf16), share)
    target = to_positions(teacher, row_parts)

    count = reduce_small(jnp.sum(lengths).astype(f32).reshape(1, 1) + jnp.zeros((8, 128), f32), ("dp",))[0, 0]
    length = lax.dynamic_index_in_dim(lengths, col, 0, False)
    keep = ((row * tokens + jnp.arange(tokens, dtype=jnp.int32)) < length).astype(f32)

    triple_weight = [rows_of(b) for b in triple_blocks]
    out_weight = jnp.concatenate([rows_of(b) for b in out_blocks], axis=1)
    up_weight = jnp.concatenate([rows_of(b) for b in up_blocks], axis=1)
    down_weight = jnp.concatenate([rows_of(b) for b in down_blocks], axis=1)

    triple = jnp.stack([dot(w, states, ((0,), (0,))) for w in triple_weight]) + triple_bias[:, :, None]
    triple = triple.reshape(cols, 3, head_local, head_width, tokens)
    split = [triple[:, p].reshape(heads, head_width, tokens) for p in range(3)]
    query_scaled = split[0] * factor
    key_scaled = split[1] * factor
    value_low = split[2].astype(bf16)

    def positive(scaled, keeper):
        exponent = jnp.einsum("hdt,hdm->hmt", scaled.astype(bf16), omega_all, preferred_element_type=f32)
        return keeper * jnp.exp(exponent - 0.5 * jnp.sum(scaled * scaled, axis=1, keepdims=True) - stabilizer)

    feat_query = positive(query_scaled, 1.0)
    feat_key = positive(key_scaled, keep)
    query_low = feat_query.astype(bf16)
    key_low = feat_key.astype(bf16)

    def over_row(kv, total):
        packed = jnp.concatenate((kv.reshape(heads * head_width, feats), total, jnp.zeros((4, feats), f32)))
        packed = packed + swap(packed.astype(bf16), "row", 1)
        packed = packed + swap(packed.astype(bf16), "row", 2)
        return packed[: heads * head_width].reshape(kv.shape), packed[heads * head_width : heads * (head_width + 1)]

    kv, key_total = over_row(
        jnp.einsum("hmt,hdt->hdm", key_low, value_low, preferred_element_type=f32), jnp.sum(feat_key, axis=2)
    )
    kv_low = kv.astype(bf16)
    total_low = key_total.astype(bf16)
    numerator = jnp.einsum("hdm,hmt->hdt", kv_low, query_low, preferred_element_type=f32)
    denominator = jnp.einsum("hm,hmt->ht", total_low, query_low, preferred_element_type=f32)
    inverse = 1.0 / denominator
    attended = numerator * inverse[:, None, :]
    attended_low = attended.astype(bf16).reshape(width, tokens)

    summed = states.astype(f32) + dot(out_weight, attended_low, ((1,), (0,))) + b_out_all[:, None]
    normed, normal1, scale1 = norm_forward(summed, gain1, shift1)
    normed_low = normed.astype(bf16)
    up = dot(up_weight, normed_low, ((0,), (0,))) + up_bias_all[:, None]
    gate = 0.5 * (1.0 + lax.erf(up * root_half))
    hidden_low = (up * gate).astype(bf16)
    slope = gate + up * inv_root_two_pi * jnp.exp(-0.5 * up * up)
    summed = normed + dot(down_weight, hidden_low, ((1,), (0,))) + b_down_all[:, None]
    output, normal2, scale2 = norm_forward(summed, gain2, shift2)
    out_result = to_features(output, row_parts)

    differ = (output - target.astype(f32)) * keep
    loss_part = jnp.sum(differ * differ)
    grad_output = (2.0 * LOSS_SCALE / (count * width)) * differ
    grad2, gain2_grad, shift2_grad = norm_backward(grad_output, normal2, scale2, gain2)
    grad2_low = grad2.astype(bf16)

    ff = up_weight.shape[1]
    w_down_grad = weight_grad(grad2_low, hidden_low.reshape(cols, ff // cols, tokens), row_parts, share)
    b_down_grad = jnp.sum(grad2_low.astype(f32), axis=1)
    grad_up_low = (dot(down_weight, grad2_low, ((0,), (0,))) * slope).astype(bf16)
    w_up_grad = weight_grad(normed_low, grad_up_low.reshape(cols, ff // cols, tokens), row_parts, share)
    b_up_grad = jnp.sum(grad_up_low.astype(f32), axis=1)
    grad_normed = grad2 + dot(up_weight, grad_up_low, ((1,), (0,)))
    grad1, gain1_grad, shift1_grad = norm_backward(grad_normed, normal1, scale1, gain1)
    grad1_low = grad1.astype(bf16)

    w_out_grad = weight_grad(grad1_low, attended_low.reshape(cols, head_block, tokens), row_parts, share)
    b_out_grad = jnp.sum(grad1_low.astype(f32), axis=1)
    grad_att = dot(out_weight, grad1_low, ((0,), (0,))).reshape(heads, head_width, tokens)
    grad_num = (grad_att * inverse[:, None, :]).astype(bf16)
    grad_den = (-jnp.sum(grad_att * attended, axis=1) * inverse).astype(bf16)
    grad_kv, grad_total = over_row(
        jnp.einsum("hmt,hdt->hdm", query_low, grad_num, preferred_element_type=f32),
        jnp.einsum("hmt,ht->hm", query_low, grad_den, preferred_element_type=f32),
    )
    grad_kv_low = grad_kv.astype(bf16)

    def feature_back(grad_feat, feat, scaled):
        grad_expo = grad_feat * feat
        back = jnp.einsum("hmt,hdm->hdt", grad_expo.astype(bf16), omega_all, preferred_element_type=f32)
        back = back - jnp.sum(grad_expo, axis=1, keepdims=True) * scaled
        return (factor * back).astype(bf16)

    grad_feat_query = jnp.einsum("hdt,hdm->hmt", grad_num, kv_low, preferred_element_type=f32)
    grad_feat_query = grad_feat_query + grad_den.astype(f32)[:, None, :] * total_low.astype(f32)[:, :, None]
    grad_query = feature_back(grad_feat_query, feat_query, query_scaled)
    grad_feat_key = jnp.einsum("hdt,hdm->hmt", value_low, grad_kv_low, preferred_element_type=f32)
    grad_feat_key = grad_feat_key + grad_total[:, :, None]
    grad_key = feature_back(grad_feat_key, feat_key, key_scaled)
    grad_value = jnp.einsum("hmt,hdm->hdt", key_low, grad_kv_low, preferred_element_type=f32) if False else jnp.einsum(
        "hdm,hmt->hdt", grad_kv_low, key_low, preferred_element_type=f32
    ).astype(bf16)
    grad_triple = jnp.stack(
        [g.reshape(cols, head_block, tokens) for g in (grad_query, grad_key, grad_value)], axis=1
    ).reshape(cols, 3 * head_block, tokens)
    w_triple_grad = weight_grad(states, grad_triple, row_parts, share)
    b_triple_grad = jnp.sum(grad_triple.astype(f32), axis=2)
    grad_input = grad1
    for i in range(cols):
        grad_input = grad_input + dot(triple_weight[i], grad_triple[i], ((1,), (0,)))
    grad_input = to_features(grad_input, row_parts)

    row_small = jnp.stack(
        (b_out_grad, gain1_grad, shift1_grad, b_down_grad, gain2_grad, shift2_grad)
    ).reshape(6, row_parts, feat_local)
    row_small = jnp.transpose(row_small, (1, 0, 2)).reshape(row_parts, 6 * feat_local)
    col_small = jnp.concatenate((b_triple_grad, b_up_grad.reshape(cols, ff // cols)), axis=1)
    got = row_small[0]
    for j in (1, 2, 3):
        got = got + swap(row_small[j], "row", j)
    got_col = col_small[0] + swap(col_small[1], "col", 1)
    got = got + swap(got, "col", 1)
    got_col = reduce_small(got_col, ("row",))
    loss_all = reduce_small(jnp.broadcast_to(loss_part.reshape(1), (128,)), ("row", "col"))
    small = reduce_small(jnp.concatenate((got, got_col, loss_all)), ("dp",))
    row_part = small[: 6 * feat_local].reshape(6, feat_local)
    col_part = small[6 * feat_local : 6 * feat_local + col_small.shape[1]]
    loss = small[-1] / (count * width)

    return (
        out_result,
        loss,
        grad_input,
        w_triple_grad[:, :head_block],
        col_part[:head_block],
        w_triple_grad[:, head_block : 2 * head_block],
        col_part[head_block : 2 * head_block],
        w_triple_grad[:, 2 * head_block :],
        col_part[2 * head_block : 3 * head_block],
        w_out_grad,
        row_part[0],
        row_part[1],
        row_part[2],
        w_up_grad,
        col_part[3 * head_block :],
        w_down_grad,
        row_part[3],
        row_part[4],
        row_part[5],
    )


def solution(mesh):
    both = P("row", ("dp", "col"))
    in_specs = (
        both, both, P("dp"), P("col", None, None),
        P("row", "col"), P("col"), P("row", "col"), P("col"), P("row", "col"), P("col"),
        P("row", "col"), P("row"), P("row"), P("row"),
        P("row", "col"), P("col"), P("row", "col"), P("row"), P("row"), P("row"),
    )
    out_specs = (
        both, P(), both,
        P("row", "col"), P("col"), P("row", "col"), P("col"), P("row", "col"), P("col"),
        P("row", "col"), P("row"), P("row"), P("row"),
        P("row", "col"), P("col"), P("row", "col"), P("row"), P("row"), P("row"),
    )
    return jax.shard_map(shards, mesh=mesh, in_specs=in_specs, out_specs=out_specs, check_vma=False)
```

time: 1470 us -> 499 us (0.34)
  waiting for transfers between devices: 1010 us -> 163 us
  blocking collectives: 200 us -> 0 us
  starting transfers between devices: 1.87 us -> 120 us
  matrix products: 133 us -> 89.7 us
  local copies, waits for them, and re-layouts: 17.2 us -> 53.7 us
  other arithmetic: 81.9 us -> 58.8 us
    reduce_scatter x8 -> x0, waiting for transfers between devices: 663 us -> none  [the longest x4 559 us: positive_product(): lax.psum_scatter(jnp.einsum(form, whole, weight, preferred_element_type=j...]
    all_gather x8 -> x0, waiting for transfers between devices: 347 us -> none  [the longest x4 237 us: pos_whole(): return lax.all_gather(segment, 'row', axis=0, tiled=True)]
    psum x12 -> x0, blocking collectives: 200 us -> none  [the longest x2 81.8 us: shards(): loss_total, count = lax.psum((loss_part, count_part), ('dp', 'row', 'col'))]
    ppermute x0 -> x111, waiting for transfers between devices: none -> 163 us  [swap(): return lax.ppermute(value, axis, [(s, s ^ mask) for s in range(size)])]
    ppermute x0 -> x111, starting transfers between devices: none -> 120 us  [swap(): return lax.ppermute(value, axis, [(s, s ^ mask) for s in range(size)])]
    dot_general x24 -> x38, matrix products: 133 us -> 89.7 us  [the longest x26 66.4 us: dot(): return lax.dot_general(a, b, (dims, ((), ())), preferred_element_type=f32)]
    convert_element_type x14 -> x20, other arithmetic: 39.4 us -> 9.32 us  [the longest x4 3.21 us: reduce_dp(): return out.reshape(value.shape).astype(f32)]
    reduce_sum x14 -> x9, other arithmetic: 31.3 us -> 7.28 us  [the longest x1 2.74 us: norm_backward(): jnp.sum(grad_out * normal, axis=1)]
  transfers between devices with their start and end apart: 17 -> 111, of which waited for: 16 -> 38; matrix products, arithmetic and copies ran while one was open for 4% -> 30% of each run, Pallas kernels for 0% -> 0%
where the time goes in v1:
time: 499 us; the launch traced here: 492 us
  waiting for transfers between devices  163 us (33%)
  starting transfers between devices  120 us (24%)
  matrix products  89.7 us (18%)
  other arithmetic  58.8 us (12%)
  local copies, waits for them, and re-layouts  53.7 us (11%)
  between operations  6.54 us (1%)
    ppermute x111, waiting for transfers between devices, swap(): return lax.ppermute(value, axis, [(s, s ^ mask) for s in range(size)])  163 us
    ppermute x111, starting transfers between devices, swap(): return lax.ppermute(value, axis, [(s, s ^ mask) for s in range(size)])  120 us
    dot_general x26, matrix products, dot(): return lax.dot_general(a, b, (dims, ((), ())), preferred_element_type=f32)  66.4 us
    another operation x8, local copies, waits for them, and re-layouts, reduce_plane(): got = swap(jnp.stack(theirs).astype(bf16), 'row', 1)  17.3 us
  transfers between devices with their start and end apart: 111, of which 38 were waited for; matrix products, arithmetic and copies ran while one was open for 30% of the time, Pallas kernels for 0%

profile of v1, /device:TPU:0, one launch (start us, length us, event | category | flops | bytes accessed | tf_op | source)
XLA Modules:
  0.0 491.9 jit_solution(7983255686574043279)
XLA Ops:
  1.6 2.5 collective-permute-start.25
  18.0 2.4 dynamic-slice_convert_fusion.3
  29.3 2.6 collective-permute-start.46
  45.1 2.5 collective-permute-done.9
  54.9 6.1 %collective-permute-done.37 = bf16[192,1536]{1,0:T(8,128)(2,1)S(1)} collective-permute-done((bf16[192,1536]{1,0:T(8,128)(2,1)}, bf16[192,1536]{1,0:T(8,128)(2,1)S(1)}, u32[]{:S(2)}, u32[]{:S(2)}) %collective-permute-start.37) | collective-permute-done | bytes 589856 | tf_op jit(solution)/shard_map/ppermute | solution.py:18
  62.5 11.1 %collective-permute-done.29 = bf16[192,1536]{1,0:T(8,128)(2,1)S(1)} collective-permute-done((bf16[192,1536]{1,0:T(8,128)(2,1)S(1)}, bf16[192,1536]{1,0:T(8,128)(2,1)S(1)}, u32[]{:S(2)}, u32[]{:S(2)}) %collective-permute-start.29) | collective-permute-done | bytes 589856 | tf_op jit(solution)/shard_map/ppermute | solution.py:18
  76.3 4.0 collective-permute-done.17
  81.8 4.2 collective-permute-done.1
  91.8 7.8 %collective-permute-done.40 = bf16[144,1536]{1,0:T(8,128)(2,1)S(1)} collective-permute-done((bf16[144,1536]{1,0:T(8,128)(2,1)S(1)}, bf16[144,1536]{1,0:T(8,128)(2,1)S(1)}, u32[]{:S(2)}, u32[]{:S(2)}) %collective-permute-start.40) | collective-permute-done | bytes 442400 | tf_op jit(solution)/shard_map/ppermute | solution.py:18
  101.9 2.8 collective-permute-done.31
  104.7 3.1 collective-permute-done.32
  125.8 3.9 fusion.5
  134.8 7.8 %collective-permute-done.22 = bf16[784,256]{1,0:T(8,128)(2,1)S(1)} collective-permute-done((bf16[784,256]{1,0:T(8,128)(2,1)S(1)}, bf16[784,256]{1,0:T(8,128)(2,1)S(1)}, u32[]{:S(2)}, u32[]{:S(2)}) %collective-permute-start.22) | collective-permute-done | bytes 401440 | tf_op jit(solution)/shard_map/ppermute | solution.py:18
  150.1 11.3 %multiply_convert_fusion = (bf16[3072,512]{0,1:T(8,128)(2,1)S(1)}, f32[3072,512]{0,1:T(8,128)}) fusion(f32[3072]{0:T(1024)S(1)} %copy-done.91, bf16[768,512]{1,0:T(8,128)(2,1)S(1)} %fusion.26, bf16[768,1536]{1,0:T(8,128)(2,1)S(1)} %constant_dynamic-update-slice_fusion.17, bf16[192,1536]{1,0:T(8,128)(2,1)S(1)} %collective-permute-done.36, ...), kind=kOutput, calls=%fused_computation.9 | convolution fusion | flops 2448949248 | bytes 14954496 | tf_op jit(solution)/shard_map/dot_general | solution.py:22
  161.5 2.8 fusion.142
  164.6 2.7 multiply_reduce_fusion.2
  168.1 10.5 %convert_reduce_fusion = (f32[3072]{0:T(1024)}, bf16[3072,512]{0,1:T(8,128)(2,1)S(1)}) fusion(f32[3072,512]{0,1:T(8,128)} %get-tuple-element.135, f32[3072]{0:T(1024)S(1)} %copy-done.91, bf16[768,512]{1,0:T(8,128)(2,1)S(1)} %get-tuple-element.63, bf16[768,1536]{1,0:T(8,128)(2,1)} %copy-done.67, bf16[192,1536]{1,0:T(8,128)(2,1)} %copy-done.105, ...), kind=kOutput, calls=%fused_computation.6 | convolution fusion | flops 2459956224 | bytes 14966784 | tf_op jit(solution)/shard_map/dot_general | solution.py:22
  178.6 10.3 %multiply_reduce_fusion.3 = (f32[768]{0:T(1024)S(1)}, f32[512]{0:T(512)S(1)}, f32[512]{0:T(512)S(1)}, f32[768]{0:T(1024)S(1)}, f32[768,512]{1,0:T(8,128)S(1)}) fusion(f32[768,512]{1,0:T(8,128)S(1)} %get-tuple-element.133, f32[512]{0:T(512)S(1)} %add_rsqrt_fusion.1, f32[512]{0:T(512)S(1)} %broadcast_multiply_fusion.9, f32[768]{0:T(1024)S(1)} %copy-done.81, ...), kind=kOutput, calls=%fused_computation.62 | convolution fusion | flops 2446587392 | bytes 14184452 | tf_op jit(solution)/shard_map/dot_general | solution.py:22
  216.0 3.6 fusion.143
  220.1 3.3 stack_reshape.33
  224.5 3.8 stack_reshape.32
  229.4 3.3 stack_reshape.35
  233.9 3.3 stack_reshape.34
  238.8 3.6 fusion.17
  273.2 7.5 %collective-permute-done.81 = bf16[48,384]{1,0:T(8,128)(2,1)S(1)} collective-permute-done((bf16[48,384]{1,0:T(8,128)(2,1)S(1)}, bf16[48,384]{1,0:T(8,128)(2,1)S(1)}, u32[]{:S(2)}, u32[]{:S(2)}) %collective-permute-start.81) | collective-permute-done | bytes 36896 | tf_op jit(solution)/shard_map/ppermute | solution.py:18
  301.6 2.9 collective-permute-done.58
  305.1 3.2 collective-permute-done.62
  322.5 3.6 collective-permute-done.87
  326.2 3.0 collective-permute-start.88
  329.2 2.7 collective-permute-done.88
  339.7 3.4 fusion.124
  345.0 2.6 fusion.120
  357.7 3.5 collective-permute-done.70
  363.5 35.5 %collective-permute-done.68 = bf16[144,1152]{1,0:T(8,128)(2,1)S(1)} collective-permute-done((bf16[144,1152]{1,0:T(8,128)(2,1)S(1)}, bf16[144,1152]{1,0:T(8,128)(2,1)S(1)}, u32[]{:S(2)}, u32[]{:S(2)}) %collective-permute-start.68) | collective-permute-done | bytes 331808 | tf_op jit(solution)/shard_map/ppermute | solution.py:18
  401.4 5.5 %collective-permute-done.71 = bf16[192,1152]{1,0:T(8,128)(2,1)S(1)} collective-permute-done((bf16[192,1152]{1,0:T(8,128)(2,1)S(1)}, bf16[192,1152]{1,0:T(8,128)(2,1)S(1)}, u32[]{:S(2)}, u32[]{:S(2)}) %collective-permute-start.71) | collective-permute-done | bytes 442400 | tf_op jit(solution)/shard_map/ppermute | solution.py:18
  408.6 16.1 %collective-permute-done.69 = bf16[192,1152]{1,0:T(8,128)(2,1)S(1)} collective-permute-done((bf16[192,1152]{1,0:T(8,128)(2,1)S(1)}, bf16[192,1152]{1,0:T(8,128)(2,1)S(1)}, u32[]{:S(2)}, u32[]{:S(2)}) %collective-permute-start.69) | collective-permute-done | bytes 442400 | tf_op jit(solution)/shard_map/ppermute | solution.py:18
  424.9 3.1 collective-permute-start.74
  429.7 3.1 collective-permute-start.96
  434.0 3.8 collective-permute-start.94
  437.8 2.3 collective-permute-start.107
  440.3 6.0 %collective-permute-start.105 = (bf16[48,1536]{1,0:T(8,128)(2,1)S(1)}, bf16[48,1536]{1,0:T(8,128)(2,1)S(1)}, u32[]{:S(2)}, u32[]{:S(2)}) collective-permute-start(bf16[48,1536]{1,0:T(8,128)(2,1)S(1)} %get-tuple-element.101), channel_id=1, source_target_pairs={{0,8},{8,0},{16,24},{24,16},{1,9},{9,1},{17,25},{25,17},{2,10},{10... | collective-permute-start | bytes 442376 | tf_op jit(solution)/shard_map/ppermute | solution.py:18
  446.3 5.1 %collective-permute-done.95 = bf16[48,1536]{1,0:T(8,128)(2,1)S(1)} collective-permute-done((bf16[48,1536]{1,0:T(8,128)(2,1)S(1)}, bf16[48,1536]{1,0:T(8,128)(2,1)S(1)}, u32[]{:S(2)}, u32[]{:S(2)}) %collective-permute-start.95) | collective-permute-done | bytes 147488 | tf_op jit(solution)/shard_map/ppermute | solution.py:18
  453.2 3.9 collective-permute-start.76
  457.3 4.1 collective-permute-done.106
  461.4 5.1 %collective-permute-start.97 = (bf16[48,1536]{1,0:T(8,128)(2,1)S(1)}, bf16[48,1536]{1,0:T(8,128)(2,1)S(1)}, u32[]{:S(2)}, u32[]{:S(2)}) collective-permute-start(bf16[48,1536]{1,0:T(8,128)(2,1)S(1)} %get-tuple-element.49), channel_id=1, source_target_pairs={{0,8},{8,0},{16,24},{24,16},{1,9},{9,1},{17,25},{25,17},{2,10},{10... | collective-permute-start | bytes 442376 | tf_op jit(solution)/shard_map/ppermute | solution.py:18
  466.5 3.4 collective-permute-start.98
  470.8 8.7 %collective-permute-start.109 = (bf16[48,1536]{1,0:T(8,128)(2,1)S(1)}, bf16[48,1536]{1,0:T(8,128)(2,1)S(1)}, u32[]{:S(2)}, u32[]{:S(2)}) collective-permute-start(bf16[48,1536]{1,0:T(8,128)(2,1)S(1)} %get-tuple-element.43), channel_id=1, source_target_pairs={{0,16},{8,24},{16,0},{24,8},{1,17},{9,25},{17,1},{25,9},{2,18},{10... | collective-permute-start | bytes 442376 | tf_op jit(solution)/shard_map/ppermute | solution.py:18
  482.1 7.2 %collective-permute-done.109 = bf16[48,1536]{1,0:T(8,128)(2,1)S(1)} collective-permute-done((bf16[48,1536]{1,0:T(8,128)(2,1)S(1)}, bf16[48,1536]{1,0:T(8,128)(2,1)S(1)}, u32[]{:S(2)}, u32[]{:S(2)}) %collective-permute-start.109) | collective-permute-done | bytes 147488 | tf_op jit(solution)/shard_map/ppermute | solution.py:18
  (675 shorter events, 220.9 us)
Async XLA Ops:
  1.6 25.7 %collective-permute-start.25 = (f32[6,192]{1,0:T(8,128)S(1)}, f32[6,192]{1,0:T(8,128)}, u32[]{:S(2)}, u32[]{:S(2)}) collective-permute-start(f32[6,192]{1,0:T(8,128)S(1)} %stack.91), channel_id=1, source_target_pairs={{0,6},{2,4},{4,2},{6,0},{1,7},{3,5},{5,3},{7,1},{8,14},{10,12},{12... | collective-permute-start | bytes 13832 | tf_op jit(solution)/shard_map/ppermute | solution.py:18
  4.0 23.8 %collective-permute-start.24 = (f32[6,192]{1,0:T(8,128)S(1)}, f32[6,192]{1,0:T(8,128)}, u32[]{:S(2)}, u32[]{:S(2)}) collective-permute-start(f32[6,192]{1,0:T(8,128)S(1)} %stack.91), channel_id=1, source_target_pairs={{0,4},{2,6},{4,0},{6,2},{1,5},{3,7},{5,1},{7,3},{8,12},{10,14},{12... | collective-permute-start | bytes 13832 | tf_op jit(solution)/shard_map/ppermute | solution.py:18
  4.7 24.7 %collective-permute-start.23 = (f32[6,192]{1,0:T(8,128)S(1)}, f32[6,192]{1,0:T(8,128)}, u32[]{:S(2)}, u32[]{:S(2)}) collective-permute-start(f32[6,192]{1,0:T(8,128)S(1)} %stack.91), channel_id=1, source_target_pairs={{0,2},{2,0},{4,6},{6,4},{1,3},{3,1},{5,7},{7,5},{8,10},{10,8},{12,... | collective-permute-start | bytes 13832 | tf_op jit(solution)/shard_map/ppermute | solution.py:18
  8.6 43.3 %collective-permute-start.14 = (bf16[192,1152]{1,0:T(8,128)(2,1)}, bf16[192,1152]{1,0:T(8,128)(2,1)S(1)}, u32[]{:S(2)}, u32[]{:S(2)}) collective-permute-start(bf16[192,1152]{1,0:T(8,128)(2,1)} %pad_maximum_fusion.16), channel_id=1, source_target_pairs={{0,1},{1,0},{2,3},{3,2},{4,5},{5,4},{6,7},{7,6},{8,9},{9,8},{10,11... | collective-permute-start | bytes 1327112 | tf_op jit(solution)/shard_map/ppermute | solution.py:18
  25.1 29.2 %collective-permute-start.12 = (bf16[192,1152]{1,0:T(8,128)(2,1)}, bf16[192,1152]{1,0:T(8,128)(2,1)S(1)}, u32[]{:S(2)}, u32[]{:S(2)}) collective-permute-start(bf16[192,1152]{1,0:T(8,128)(2,1)} %pad_maximum_fusion.16), channel_id=1, source_target_pairs={{0,4},{2,6},{4,0},{6,2},{1,5},{3,7},{5,1},{7,3},{8,12},{10,14},{12... | collective-permute-start | bytes 1327112 | tf_op jit(solution)/shard_map/ppermute | solution.py:18
  27.3 17.1 %collective-permute-start.20 = (bf16[6,64,256]{2,1,0:T(8,128)(2,1)S(1)}, bf16[6,64,256]{2,1,0:T(8,128)(2,1)S(1)}, u32[]{:S(2)}, u32[]{:S(2)}) collective-permute-start(bf16[6,64,256]{2,1,0:T(8,128)(2,1)S(1)} %copy-done.58), channel_id=1, source_target_pairs={{0,1},{1,0},{2,3},{3,2},{4,5},{5,4},{6,7},{7,6},{8,9},{9,8},{10,11... | collective-permute-start | bytes 589832 | tf_op jit(solution)/shard_map/ppermute | solution.py:18
  47.6 26.2 %collective-permute-start.35 = (bf16[192,1536]{1,0:T(8,128)(2,1)}, bf16[192,1536]{1,0:T(8,128)(2,1)S(1)}, u32[]{:S(2)}, u32[]{:S(2)}) collective-permute-start(bf16[192,1536]{1,0:T(8,128)(2,1)} %convert_element_type.404), channel_id=1, source_target_pairs={{0,4},{2,6},{4,0},{6,2},{1,5},{3,7},{5,1},{7,3},{8,12},{10,14},{12... | collective-permute-start | bytes 1769480 | tf_op jit(solution)/shard_map/ppermute | solution.py:18
  49.6 24.0 %collective-permute-start.29 = (bf16[192,1536]{1,0:T(8,128)(2,1)S(1)}, bf16[192,1536]{1,0:T(8,128)(2,1)S(1)}, u32[]{:S(2)}, u32[]{:S(2)}) collective-permute-start(bf16[192,1536]{1,0:T(8,128)(2,1)S(1)} %convert_element_type.403), channel_id=1, source_target_pairs={{0,1},{1,0},{2,3},{3,2},{4,5},{5,4},{6,7},{7,6},{8,9},{9,8},{10,11... | collective-permute-start | bytes 1769480 | tf_op jit(solution)/shard_map/ppermute | solution.py:18
  52.7 21.9 %collective-permute-start.27 = (bf16[192,1536]{1,0:T(8,128)(2,1)S(1)}, bf16[192,1536]{1,0:T(8,128)(2,1)S(1)}, u32[]{:S(2)}, u32[]{:S(2)}) collective-permute-start(bf16[192,1536]{1,0:T(8,128)(2,1)S(1)} %convert_element_type.403), channel_id=1, source_target_pairs={{0,4},{2,6},{4,0},{6,2},{1,5},{3,7},{5,1},{7,3},{8,12},{10,14},{12... | collective-permute-start | bytes 1769480 | tf_op jit(solution)/shard_map/ppermute | solution.py:18
  54.3 21.5 %collective-permute-start.16 = (bf16[48,1152]{1,0:T(8,128)(2,1)S(1)}, bf16[48,1152]{1,0:T(8,128)(2,1)S(1)}, u32[]{:S(2)}, u32[]{:S(2)}) collective-permute-start(bf16[48,1152]{1,0:T(8,128)(2,1)S(1)} %slice.590), channel_id=1, source_target_pairs={{0,4},{2,6},{4,0},{6,2},{1,5},{3,7},{5,1},{7,3},{8,12},{10,14},{12... | collective-permute-start | bytes 331784 | tf_op jit(solution)/shard_map/ppermute | solution.py:18
  61.0 19.3 %collective-permute-start.17 = (bf16[144,1152]{1,0:T(8,128)(2,1)S(1)}, bf16[144,1152]{1,0:T(8,128)(2,1)S(1)}, u32[]{:S(2)}, u32[]{:S(2)}) collective-permute-start(bf16[144,1152]{1,0:T(8,128)(2,1)S(1)} %slice.591), channel_id=1, source_target_pairs={{0,1},{1,0},{2,3},{3,2},{4,5},{5,4},{6,7},{7,6},{8,9},{9,8},{10,11... | collective-permute-start | bytes 995336 | tf_op jit(solution)/shard_map/ppermute | solution.py:18
  81.7 62.6 %collective-permute-start.3 = (bf16[192,384]{1,0:T(8,128)(2,1)}, bf16[192,384]{1,0:T(8,128)(2,1)}, u32[]{:S(2)}, u32[]{:S(2)}) collective-permute-start(bf16[192,384]{1,0:T(8,128)(2,1)} %convert_element_type.390), channel_id=1, source_target_pairs={{0,2},{2,0},{4,6},{6,4},{1,3},{3,1},{5,7},{7,5},{8,10},{10,8},{12,... | collective-permute-start | bytes 442376 | tf_op jit(solution)/shard_map/ppermute | solution.py:18
  88.1 19.7 %collective-permute-start.32 = (bf16[144,1536]{1,0:T(8,128)(2,1)S(1)}, bf16[144,1536]{1,0:T(8,128)(2,1)S(1)}, u32[]{:S(2)}, u32[]{:S(2)}) collective-permute-start(bf16[144,1536]{1,0:T(8,128)(2,1)S(1)} %slice.599), channel_id=1, source_target_pairs={{0,1},{1,0},{2,3},{3,2},{4,5},{5,4},{6,7},{7,6},{8,9},{9,8},{10,11... | collective-permute-start | bytes 1327112 | tf_op jit(solution)/shard_map/ppermute | solution.py:18
  88.6 20.1 %collective-permute-start.38 = (bf16[192,1536]{1,0:T(8,128)(2,1)S(1)}, bf16[192,1536]{1,0:T(8,128)(2,1)S(1)}, u32[]{:S(2)}, u32[]{:S(2)}) collective-permute-start(bf16[192,1536]{1,0:T(8,128)(2,1)S(1)} %collective-permute-done.37), channel_id=1, source_target_pairs={{0,2},{2,0},{4,6},{6,4},{1,3},{3,1},{5,7},{7,5},{8,10},{10,8},{12,... | collective-permute-start | bytes 1769480 | tf_op jit(solution)/shard_map/ppermute | solution.py:18
  91.7 57.0 %collective-permute-start.34 = (bf16[192,1536]{1,0:T(8,128)(2,1)}, bf16[192,1536]{1,0:T(8,128)(2,1)}, u32[]{:S(2)}, u32[]{:S(2)}) collective-permute-start(bf16[192,1536]{1,0:T(8,128)(2,1)} %convert_element_type.404), channel_id=1, source_target_pairs={{0,2},{2,0},{4,6},{6,4},{1,3},{3,1},{5,7},{7,5},{8,10},{10,8},{12,... | collective-permute-start | bytes 1769480 | tf_op jit(solution)/shard_map/ppermute | solution.py:18
  108.7 21.7 %collective-permute-start.41 = (bf16[192,1536]{1,0:T(8,128)(2,1)}, bf16[192,1536]{1,0:T(8,128)(2,1)}, u32[]{:S(2)}, u32[]{:S(2)}) collective-permute-start(bf16[192,1536]{1,0:T(8,128)(2,1)} %pad_maximum_fusion.10), channel_id=1, source_target_pairs={{0,2},{2,0},{4,6},{6,4},{1,3},{3,1},{5,7},{7,5},{8,10},{10,8},{12,... | collective-permute-start | bytes 1769480 | tf_op jit(solution)/shard_map/ppermute | solution.py:18
  109.3 23.8 %collective-permute-start.33 = (bf16[192,1536]{1,0:T(8,128)(2,1)}, bf16[192,1536]{1,0:T(8,128)(2,1)}, u32[]{:S(2)}, u32[]{:S(2)}) collective-permute-start(bf16[192,1536]{1,0:T(8,128)(2,1)} %pad_maximum_fusion.9), channel_id=1, source_target_pairs={{0,2},{2,0},{4,6},{6,4},{1,3},{3,1},{5,7},{7,5},{8,10},{10,8},{12,... | collective-permute-start | bytes 1769480 | tf_op jit(solution)/shard_map/ppermute | solution.py:18
  129.7 31.7 %collective-permute-start.26 = (bf16[192,1536]{1,0:T(8,128)(2,1)S(1)}, bf16[192,1536]{1,0:T(8,128)(2,1)S(1)}, u32[]{:S(2)}, u32[]{:S(2)}) collective-permute-start(bf16[192,1536]{1,0:T(8,128)(2,1)S(1)} %copy-done.32), channel_id=1, source_target_pairs={{0,2},{2,0},{4,6},{6,4},{1,3},{3,1},{5,7},{7,5},{8,10},{10,8},{12,... | collective-permute-start | bytes 1769480 | tf_op jit(solution)/shard_map/ppermute | solution.py:18
  133.1 31.4 %collective-permute-start.49 = (bf16[192,512]{1,0:T(8,128)(2,1)S(1)}, bf16[192,512]{1,0:T(8,128)(2,1)S(1)}, u32[]{:S(2)}, u32[]{:S(2)}) collective-permute-start(bf16[192,512]{1,0:T(8,128)(2,1)S(1)} %copy-done.53), channel_id=1, source_target_pairs={{0,6},{2,4},{4,2},{6,0},{1,7},{3,5},{5,3},{7,1},{8,14},{10,12},{12... | collective-permute-start | bytes 589832 | tf_op jit(solution)/shard_map/ppermute | solution.py:18
  144.5 20.1 %collective-permute-start.48 = (bf16[192,512]{1,0:T(8,128)(2,1)S(1)}, bf16[192,512]{1,0:T(8,128)(2,1)S(1)}, u32[]{:S(2)}, u32[]{:S(2)}) collective-permute-start(bf16[192,512]{1,0:T(8,128)(2,1)S(1)} %copy-done.52), channel_id=1, source_target_pairs={{0,4},{2,6},{4,0},{6,2},{1,5},{3,7},{5,1},{7,3},{8,12},{10,14},{12... | collective-permute-start | bytes 589832 | tf_op jit(solution)/shard_map/ppermute | solution.py:18
  209.6 53.0 %collective-permute-start.42 = (bf16[192,512]{1,0:T(8,128)(2,1)}, bf16[192,512]{1,0:T(8,128)(2,1)}, u32[]{:S(2)}, u32[]{:S(2)}) collective-permute-start(bf16[192,512]{1,0:T(8,128)(2,1)} %get-tuple-element.100), channel_id=1, source_target_pairs={{0,2},{2,0},{4,6},{6,4},{1,3},{3,1},{5,7},{7,5},{8,10},{10,8},{12,... | collective-permute-start | bytes 589832 | tf_op jit(solution)/shard_map/ppermute | solution.py:18
  209.9 54.6 %collective-permute-start.43 = (bf16[192,512]{1,0:T(8,128)(2,1)}, bf16[192,512]{1,0:T(8,128)(2,1)}, u32[]{:S(2)}, u32[]{:S(2)}) collective-permute-start(bf16[192,512]{1,0:T(8,128)(2,1)} %get-tuple-element.99), channel_id=1, source_target_pairs={{0,4},{2,6},{4,0},{6,2},{1,5},{3,7},{5,1},{7,3},{8,12},{10,14},{12... | collective-permute-start | bytes 589832 | tf_op jit(solution)/shard_map/ppermute | solution.py:18
  211.5 35.5 %collective-permute-start.59 = (f32[128]{0:T(128)}, f32[128]{0:T(128)}, u32[]{:S(2)}, u32[]{:S(2)}) collective-permute-start(f32[128]{0:T(128)} %broadcast_in_dim.83), channel_id=1, source_target_pairs={{0,2},{2,0},{4,6},{6,4},{1,3},{3,1},{5,7},{7,5},{8,10},{10,8},{12,... | collective-permute-start | bytes 1544 | tf_op jit(solution)/shard_map/ppermute | solution.py:18
  262.7 77.0 %collective-permute-start.89 = (bf16[2,192,2,1536]{3,1,2,0:T(8,128)(2,1)}, bf16[2,192,2,1536]{3,1,2,0:T(8,128)(2,1)}, u32[]{:S(2)}, u32[]{:S(2)}) collective-permute-start(bf16[2,192,2,1536]{3,1,2,0:T(8,128)(2,1)} %pad_maximum_fusion.3), channel_id=1, source_target_pairs={{0,2},{2,0},{4,6},{6,4},{1,3},{3,1},{5,7},{7,5},{8,10},{10,8},{12,... | collective-permute-start | bytes 7077896 | tf_op jit(solution)/shard_map/ppermute | solution.py:18
  264.5 80.5 %collective-permute-start.100 = (bf16[2,192,2,1536]{3,1,2,0:T(8,128)(2,1)}, bf16[2,192,2,1536]{3,1,2,0:T(8,128)(2,1)}, u32[]{:S(2)}, u32[]{:S(2)}) collective-permute-start(bf16[2,192,2,1536]{3,1,2,0:T(8,128)(2,1)} %pad_maximum_fusion.4), channel_id=1, source_target_pairs={{0,2},{2,0},{4,6},{6,4},{1,3},{3,1},{5,7},{7,5},{8,10},{10,8},{12,... | collective-permute-start | bytes 7077896 | tf_op jit(solution)/shard_map/ppermute | solution.py:18
  280.7 24.3 %collective-permute-start.82 = (bf16[192,384]{1,0:T(8,128)(2,1)S(1)}, bf16[192,384]{1,0:T(8,128)(2,1)S(1)}, u32[]{:S(2)}, u32[]{:S(2)}) collective-permute-start(bf16[192,384]{1,0:T(8,128)(2,1)S(1)} %pad_maximum_fusion.22), channel_id=1, source_target_pairs={{0,1},{1,0},{2,3},{3,2},{4,5},{5,4},{6,7},{7,6},{8,9},{9,8},{10,11... | collective-permute-start | bytes 442376 | tf_op jit(solution)/shard_map/ppermute | solution.py:18
  282.4 22.6 %collective-permute-start.80 = (bf16[192,384]{1,0:T(8,128)(2,1)S(1)}, bf16[192,384]{1,0:T(8,128)(2,1)S(1)}, u32[]{:S(2)}, u32[]{:S(2)}) collective-permute-start(bf16[192,384]{1,0:T(8,128)(2,1)S(1)} %pad_maximum_fusion.21), channel_id=1, source_target_pairs={{0,4},{2,6},{4,0},{6,2},{1,5},{3,7},{5,1},{7,3},{8,12},{10,14},{12... | collective-permute-start | bytes 442376 | tf_op jit(solution)/shard_map/ppermute | solution.py:18
  315.7 17.0 %collective-permute-start.64 = (bf16[192,512]{1,0:T(8,128)(2,1)}, bf16[192,512]{1,0:T(8,128)(2,1)}, u32[]{:S(2)}, u32[]{:S(2)}) collective-permute-start(bf16[192,512]{1,0:T(8,128)(2,1)} %get-tuple-element.97), channel_id=1, source_target_pairs={{0,2},{2,0},{4,6},{6,4},{1,3},{3,1},{5,7},{7,5},{8,10},{10,8},{12,... | collective-permute-start | bytes 589832 | tf_op jit(solution)/shard_map/ppermute | solution.py:18
  316.5 19.7 %collective-permute-start.65 = (bf16[192,512]{1,0:T(8,128)(2,1)S(1)}, bf16[192,512]{1,0:T(8,128)(2,1)}, u32[]{:S(2)}, u32[]{:S(2)}) collective-permute-start(bf16[192,512]{1,0:T(8,128)(2,1)S(1)} %get-tuple-element.96), channel_id=1, source_target_pairs={{0,4},{2,6},{4,0},{6,2},{1,5},{3,7},{5,1},{7,3},{8,12},{10,14},{12... | collective-permute-start | bytes 589832 | tf_op jit(solution)/shard_map/ppermute | solution.py:18
  332.7 21.7 %collective-permute-start.67 = (bf16[2,192,2,1152]{3,1,2,0:T(8,128)(2,1)}, bf16[2,192,2,1152]{3,1,2,0:T(8,128)(2,1)S(1)}, u32[]{:S(2)}, u32[]{:S(2)}) collective-permute-start(bf16[2,192,2,1152]{3,1,2,0:T(8,128)(2,1)} %pad_maximum_fusion.6), channel_id=1, source_target_pairs={{0,2},{2,0},{4,6},{6,4},{1,3},{3,1},{5,7},{7,5},{8,10},{10,8},{12,... | collective-permute-start | bytes 5308424 | tf_op jit(solution)/shard_map/ppermute | solution.py:18
  344.0 18.4 %collective-permute-start.90 = (bf16[144,1536]{1,0:T(8,128)(2,1)S(1)}, bf16[144,1536]{1,0:T(8,128)(2,1)S(1)}, u32[]{:S(2)}, u32[]{:S(2)}) collective-permute-start(bf16[144,1536]{1,0:T(8,128)(2,1)S(1)} %slice_bitcast_fusion.13), channel_id=1, source_target_pairs={{0,1},{1,0},{2,3},{3,2},{4,5},{5,4},{6,7},{7,6},{8,9},{9,8},{10,11... | collective-permute-start | bytes 1327112 | tf_op jit(solution)/shard_map/ppermute | solution.py:18
  349.0 51.3 %collective-permute-start.101 = (bf16[144,1536]{1,0:T(8,128)(2,1)S(1)}, bf16[144,1536]{1,0:T(8,128)(2,1)S(1)}, u32[]{:S(2)}, u32[]{:S(2)}) collective-permute-start(bf16[144,1536]{1,0:T(8,128)(2,1)S(1)} %slice_bitcast_fusion.12), channel_id=1, source_target_pairs={{0,1},{1,0},{2,3},{3,2},{4,5},{5,4},{6,7},{7,6},{8,9},{9,8},{10,11... | collective-permute-start | bytes 1327112 | tf_op jit(solution)/shard_map/ppermute | solution.py:18
  350.3 77.7 %collective-permute-start.93 = (bf16[192,1536]{1,0:T(8,128)(2,1)S(1)}, bf16[192,1536]{1,0:T(8,128)(2,1)S(1)}, u32[]{:S(2)}, u32[]{:S(2)}) collective-permute-start(bf16[192,1536]{1,0:T(8,128)(2,1)S(1)} %pad_maximum_fusion.13), channel_id=1, source_target_pairs={{0,1},{1,0},{2,3},{3,2},{4,5},{5,4},{6,7},{7,6},{8,9},{9,8},{10,11... | collective-permute-start | bytes 1769480 | tf_op jit(solution)/shard_map/ppermute | solution.py:18
  353.5 76.2 %collective-permute-start.104 = (bf16[192,1536]{1,0:T(8,128)(2,1)S(1)}, bf16[192,1536]{1,0:T(8,128)(2,1)S(1)}, u32[]{:S(2)}, u32[]{:S(2)}) collective-permute-start(bf16[192,1536]{1,0:T(8,128)(2,1)S(1)} %pad_maximum_fusion.15), channel_id=1, source_target_pairs={{0,1},{1,0},{2,3},{3,2},{4,5},{5,4},{6,7},{7,6},{8,9},{9,8},{10,11... | collective-permute-start | bytes 1769480 | tf_op jit(solution)/shard_map/ppermute | solution.py:18
  361.2 37.8 %collective-permute-start.68 = (bf16[144,1152]{1,0:T(8,128)(2,1)S(1)}, bf16[144,1152]{1,0:T(8,128)(2,1)S(1)}, u32[]{:S(2)}, u32[]{:S(2)}) collective-permute-start(bf16[144,1152]{1,0:T(8,128)(2,1)S(1)} %slice_bitcast_fusion.14), channel_id=1, source_target_pairs={{0,1},{1,0},{2,3},{3,2},{4,5},{5,4},{6,7},{7,6},{8,9},{9,8},{10,11... | collective-permute-start | bytes 995336 | tf_op jit(solution)/shard_map/ppermute | solution.py:18
  362.5 44.4 %collective-permute-start.71 = (bf16[192,1152]{1,0:T(8,128)(2,1)S(1)}, bf16[192,1152]{1,0:T(8,128)(2,1)S(1)}, u32[]{:S(2)}, u32[]{:S(2)}) collective-permute-start(bf16[192,1152]{1,0:T(8,128)(2,1)S(1)} %pad_maximum_fusion.19), channel_id=1, source_target_pairs={{0,1},{1,0},{2,3},{3,2},{4,5},{5,4},{6,7},{7,6},{8,9},{9,8},{10,11... | collective-permute-start | bytes 1327112 | tf_op jit(solution)/shard_map/ppermute | solution.py:18
  399.0 29.0 %collective-permute-start.91 = (bf16[192,1536]{1,0:T(8,128)(2,1)S(1)}, bf16[192,1536]{1,0:T(8,128)(2,1)S(1)}, u32[]{:S(2)}, u32[]{:S(2)}) collective-permute-start(bf16[192,1536]{1,0:T(8,128)(2,1)S(1)} %pad_maximum_fusion.12), channel_id=1, source_target_pairs={{0,4},{2,6},{4,0},{6,2},{1,5},{3,7},{5,1},{7,3},{8,12},{10,14},{12... | collective-permute-start | bytes 1769480 | tf_op jit(solution)/shard_map/ppermute | solution.py:18
  400.4 24.3 %collective-permute-start.69 = (bf16[192,1152]{1,0:T(8,128)(2,1)S(1)}, bf16[192,1152]{1,0:T(8,128)(2,1)S(1)}, u32[]{:S(2)}, u32[]{:S(2)}) collective-permute-start(bf16[192,1152]{1,0:T(8,128)(2,1)S(1)} %pad_maximum_fusion.18), channel_id=1, source_target_pairs={{0,4},{2,6},{4,0},{6,2},{1,5},{3,7},{5,1},{7,3},{8,12},{10,14},{12... | collective-permute-start | bytes 1327112 | tf_op jit(solution)/shard_map/ppermute | solution.py:18
  406.9 26.8 %collective-permute-start.102 = (bf16[192,1536]{1,0:T(8,128)(2,1)S(1)}, bf16[192,1536]{1,0:T(8,128)(2,1)S(1)}, u32[]{:S(2)}, u32[]{:S(2)}) collective-permute-start(bf16[192,1536]{1,0:T(8,128)(2,1)S(1)} %pad_maximum_fusion.14), channel_id=1, source_target_pairs={{0,4},{2,6},{4,0},{6,2},{1,5},{3,7},{5,1},{7,3},{8,12},{10,14},{12... | collective-permute-start | bytes 1769480 | tf_op jit(solution)/shard_map/ppermute | solution.py:18
  433.7 17.7 %collective-permute-start.95 = (bf16[48,1536]{1,0:T(8,128)(2,1)S(1)}, bf16[48,1536]{1,0:T(8,128)(2,1)S(1)}, u32[]{:S(2)}, u32[]{:S(2)}) collective-permute-start(bf16[48,1536]{1,0:T(8,128)(2,1)S(1)} %get-tuple-element.106), channel_id=1, source_target_pairs={{0,16},{8,24},{16,0},{24,8},{1,17},{9,25},{17,1},{25,9},{2,18},{10... | collective-permute-start | bytes 442376 | tf_op jit(solution)/shard_map/ppermute | solution.py:18
  434.0 19.3 %collective-permute-start.94 = (bf16[48,1536]{1,0:T(8,128)(2,1)S(1)}, bf16[48,1536]{1,0:T(8,128)(2,1)S(1)}, u32[]{:S(2)}, u32[]{:S(2)}) collective-permute-start(bf16[48,1536]{1,0:T(8,128)(2,1)S(1)} %get-tuple-element.104), channel_id=1, source_target_pairs={{0,8},{8,0},{16,24},{24,16},{1,9},{9,1},{17,25},{25,17},{2,10},{10... | collective-permute-start | bytes 442376 | tf_op jit(solution)/shard_map/ppermute | solution.py:18
  437.8 19.4 %collective-permute-start.107 = (bf16[48,1536]{1,0:T(8,128)(2,1)S(1)}, bf16[48,1536]{1,0:T(8,128)(2,1)S(1)}, u32[]{:S(2)}, u32[]{:S(2)}) collective-permute-start(bf16[48,1536]{1,0:T(8,128)(2,1)S(1)} %get-tuple-element.102), channel_id=1, source_target_pairs={{0,24},{8,16},{16,8},{24,0},{1,25},{9,17},{17,9},{25,1},{2,26},{10... | collective-permute-start | bytes 442376 | tf_op jit(solution)/shard_map/ppermute | solution.py:18
  440.2 21.2 %collective-permute-start.106 = (bf16[48,1536]{1,0:T(8,128)(2,1)S(1)}, bf16[48,1536]{1,0:T(8,128)(2,1)S(1)}, u32[]{:S(2)}, u32[]{:S(2)}) collective-permute-start(bf16[48,1536]{1,0:T(8,128)(2,1)S(1)} %get-tuple-element.103), channel_id=1, source_target_pairs={{0,16},{8,24},{16,0},{24,8},{1,17},{9,25},{17,1},{25,9},{2,18},{10... | collective-permute-start | bytes 442376 | tf_op jit(solution)/shard_map/ppermute | solution.py:18
  440.3 26.2 %collective-permute-start.105 = (bf16[48,1536]{1,0:T(8,128)(2,1)S(1)}, bf16[48,1536]{1,0:T(8,128)(2,1)S(1)}, u32[]{:S(2)}, u32[]{:S(2)}) collective-permute-start(bf16[48,1536]{1,0:T(8,128)(2,1)S(1)} %get-tuple-element.101), channel_id=1, source_target_pairs={{0,8},{8,0},{16,24},{24,16},{1,9},{9,1},{17,25},{25,17},{2,10},{10... | collective-permute-start | bytes 442376 | tf_op jit(solution)/shard_map/ppermute | solution.py:18
  451.4 18.6 %collective-permute-start.75 = (bf16[48,1152]{1,0:T(8,128)(2,1)S(1)}, bf16[48,1152]{1,0:T(8,128)(2,1)S(1)}, u32[]{:S(2)}, u32[]{:S(2)}) collective-permute-start(bf16[48,1152]{1,0:T(8,128)(2,1)S(1)} %get-tuple-element.59), channel_id=1, source_target_pairs={{0,8},{8,0},{16,24},{24,16},{1,9},{9,1},{17,25},{25,17},{2,10},{10... | collective-permute-start | bytes 331784 | tf_op jit(solution)/shard_map/ppermute | solution.py:18
  453.2 16.9 %collective-permute-start.76 = (bf16[48,1152]{1,0:T(8,128)(2,1)S(1)}, bf16[48,1152]{1,0:T(8,128)(2,1)S(1)}, u32[]{:S(2)}, u32[]{:S(2)}) collective-permute-start(bf16[48,1152]{1,0:T(8,128)(2,1)S(1)} %get-tuple-element.59), channel_id=1, source_target_pairs={{0,16},{8,24},{16,0},{24,8},{1,17},{9,25},{17,1},{25,9},{2,18},{10... | collective-permute-start | bytes 331784 | tf_op jit(solution)/shard_map/ppermute | solution.py:18
  461.4 19.2 %collective-permute-start.97 = (bf16[48,1536]{1,0:T(8,128)(2,1)S(1)}, bf16[48,1536]{1,0:T(8,128)(2,1)S(1)}, u32[]{:S(2)}, u32[]{:S(2)}) collective-permute-start(bf16[48,1536]{1,0:T(8,128)(2,1)S(1)} %get-tuple-element.49), channel_id=1, source_target_pairs={{0,8},{8,0},{16,24},{24,16},{1,9},{9,1},{17,25},{25,17},{2,10},{10... | collective-permute-start | bytes 442376 | tf_op jit(solution)/shard_map/ppermute | solution.py:18
  470.8 18.5 %collective-permute-start.109 = (bf16[48,1536]{1,0:T(8,128)(2,1)S(1)}, bf16[48,1536]{1,0:T(8,128)(2,1)S(1)}, u32[]{:S(2)}, u32[]{:S(2)}) collective-permute-start(bf16[48,1536]{1,0:T(8,128)(2,1)S(1)} %get-tuple-element.43), channel_id=1, source_target_pairs={{0,16},{8,24},{16,0},{24,8},{1,17},{9,25},{17,1},{25,9},{2,18},{10... | collective-permute-start | bytes 442376 | tf_op jit(solution)/shard_map/ppermute | solution.py:18
  (180 other events, 1467.8 us)

commit v2 on v1

--- a/solution.py
+++ b/solution.py
@@ -24,26 +24,24 @@
 
 def gather_plane(own, share):
     cut = own.shape[0] * share // 4
-    by_core = swap(own, "row", 1)
     by_x = swap(own, "row", 2)
     by_y = swap(own, "col", 1)
-    far_x = swap(by_y[:cut], "row", 2)
-    far_y = swap(by_x[cut:], "col", 1)
-    far = jnp.concatenate((far_x, far_y), axis=0)
-    x_core = swap(by_x, "row", 1)
-    y_core = swap(by_y, "row", 1)
-    far_core = swap(far, "row", 1)
-    return ((own, by_core, by_x, x_core), (by_y, y_core, far, far_core))
-
-
-def rows_of(blocks):
-    return jnp.concatenate(blocks, axis=0)
+    far = swap(by_x[cut:], "col", 1)
+    if cut:
+        far = jnp.concatenate((swap(by_y[:cut], "row", 2), far), axis=0)
+    near = jnp.concatenate((own, by_x), axis=0)
+    other = jnp.concatenate((by_y, far), axis=0)
+    return (
+        jnp.concatenate((near, swap(near, "row", 1)), axis=0),
+        jnp.concatenate((other, swap(other, "row", 1)), axis=0),
+    )
 
 
 def reduce_plane(mine, theirs, share):
-    got = swap(jnp.stack(theirs).astype(bf16), "row", 1)
-    near = mine[0] + got[0]
-    far = mine[1] + got[1]
+    got = swap(theirs.astype(bf16), "row", 1)
+    total = mine + got
+    near = total[0]
+    far = total[1]
     cut = near.shape[0] * share // 4
     far_low = far[:, 1].astype(bf16)
     from_x = swap(far_low[:cut], "row", 2)
@@ -62,17 +60,13 @@
     if parts != 4:
         return lax.psum(value.astype(bf16), "dp").astype(f32)
     index = lax.axis_index("dp")
-    n = value.shape[0] // parts
-    low = value.astype(bf16).reshape(parts, n, value.shape[1])
-    total = lax.dynamic_index_in_dim(value.reshape(low.shape), index, 0, False)
-    for mask in (1, 2, 3):
-        total = total + swap(lax.dynamic_index_in_dim(low, index ^ mask, 0, False), "dp", mask)
-    total = total.astype(bf16)
-    out = jnp.zeros(low.shape, bf16)
-    out = lax.dynamic_update_index_in_dim(out, total, index, 0)
-    for mask in (1, 2, 3):
-        out = lax.dynamic_update_index_in_dim(out, swap(total, "dp", mask), index ^ mask, 0)
-    return out.reshape(value.shape).astype(f32)
+    middle = jnp.logical_or(index == 1, index == 2)
+    low = value.astype(bf16)
+    value = value + lax.ppermute(low, "dp", [(0, 1), (3, 2)])
+    other = lax.ppermute(value.astype(bf16), "dp", [(1, 2), (2, 1)])
+    low = (value + other).astype(bf16)
+    back = lax.ppermute(low, "dp", [(1, 0), (2, 3)])
+    return jnp.where(middle, low, back).astype(f32)
 
 
 def reduce_small(value, axes):
@@ -84,31 +78,36 @@
     return value
 
 
+ORDER = (0, 2, 1, 3)
+
+
 def to_positions(shard, row_parts):
     row = lax.axis_index("row")
+    k = shard.shape[0]
     n = shard.shape[1] // row_parts
-    blocks = []
-    for j in range(row_parts):
-        block = lax.dynamic_slice_in_dim(shard, (row ^ j) * n, n, 1).astype(bf16)
-        blocks.append(swap(block, "row", j) if j else block)
-    return jnp.concatenate(blocks, axis=0)
+    blocks = [lax.dynamic_slice_in_dim(shard, (row ^ j) * n, n, 1).astype(bf16) for j in range(4)]
+    got = swap(jnp.concatenate((blocks[1], blocks[3]), axis=0), "row", 1)
+    here = jnp.concatenate((blocks[0], got[:k]), axis=0)
+    there = swap(jnp.concatenate((blocks[2], got[k:]), axis=0), "row", 2)
+    return jnp.concatenate((here[:k], there[:k], here[k:], there[k:]), axis=0)
 
 
 def to_features(value, row_parts):
     row = lax.axis_index("row")
     k = value.shape[0] // row_parts
     n = value.shape[1]
+    low = value.astype(bf16)
+    got = swap(jnp.concatenate((low[k : 2 * k], low[3 * k :]), axis=0), "row", 2)
+    core = swap(jnp.concatenate((low[2 * k : 3 * k], got[k:]), axis=0), "row", 1)
     out = jnp.zeros((k, n * row_parts), f32)
-    for j in range(row_parts):
-        block = value[j * k : (j + 1) * k]
-        if j:
-            block = swap(block.astype(bf16), "row", j).astype(f32)
-        out = lax.dynamic_update_slice_in_dim(out, block, (row ^ j) * n, 1)
+    for j, block in ((0, value[:k]), (2, got[:k]), (1, core[:k]), (3, core[k:])):
+        out = lax.dynamic_update_slice_in_dim(out, block.astype(f32), (row ^ j) * n, 1)
     return out
 
 
 def row_vectors(packed):
-    return jnp.concatenate([packed] + [swap(packed, "row", j) for j in (1, 2, 3)], axis=1)
+    got = jnp.concatenate((packed, swap(packed, "row", 2)), axis=1)
+    return jnp.concatenate((got, swap(got, "row", 1)), axis=1)
 
 
 def norm_forward(summed, gain, shift):
@@ -128,15 +127,17 @@
     return grad_in, jnp.sum(grad_out * normal, axis=1), jnp.sum(grad_out, axis=1)
 
 
-def weight_grad(left, right, row_parts, share):
+def partial_grad(left, right, row_parts):
     n = left.shape[0] // row_parts
-    cols, k, _ = right.shape
-    flat = right.reshape(cols * k, -1)
-    parts = [
-        dot(left[j * n : (j + 1) * n], flat, ((1,), (1,))).reshape(n, cols, k)
-        for j in range(row_parts)
-    ]
-    return reduce_dp(reduce_plane(parts[0::2], parts[1::2], share))
+    cols, k, tokens = right.shape
+    flat = right.reshape(cols * k, tokens)
+    theirs = dot(left[2 * n :], flat, ((1,), (1,))).reshape(2, n, cols, k)
+    mine = dot(left[: 2 * n], flat, ((1,), (1,))).reshape(2, n, cols, k)
+    return mine, theirs
+
+
+def finish_grad(parts, share):
+    return reduce_dp(reduce_plane(*parts, share))
 
 
 def shards(
@@ -159,7 +160,7 @@
 
     own_triple = jnp.concatenate((w_query, w_key, w_value), axis=1).astype(bf16)
     states = to_positions(inputs, row_parts)
-    triple_blocks = gather_plane(own_triple, share)
+    triple_weight = gather_plane(own_triple, 0)
     omega_all = jnp.concatenate((omega, swap(omega, "col", 1)), axis=0)
     col_pack = jnp.concatenate((b_query, b_key, b_value, up_bias))
     col_other = swap(col_pack, "col", 1)
@@ -167,19 +168,17 @@
     b_out_all, gain1, shift1, b_down_all, gain2, shift2 = [row_pack[m] for m in range(6)]
     triple_bias = jnp.stack((col_pack[: 3 * head_block], col_other[: 3 * head_block]))
     up_bias_all = jnp.concatenate((col_pack[3 * head_block :], col_other[3 * head_block :]))
-    out_blocks = gather_plane(w_out.astype(bf16), share)
-    up_blocks = gather_plane(w_up.astype(bf16), share)
-    down_blocks = gather_plane(w_down.astype(bf16), share)
+    rest = gather_plane(jnp.concatenate((w_out, w_up, w_down), axis=1).astype(bf16), share)
     target = to_positions(teacher, row_parts)
 
     count = reduce_small(jnp.sum(lengths).astype(f32).reshape(1, 1) + jnp.zeros((8, 128), f32), ("dp",))[0, 0]
     length = lax.dynamic_index_in_dim(lengths, col, 0, False)
     keep = ((row * tokens + jnp.arange(tokens, dtype=jnp.int32)) < length).astype(f32)
 
-    triple_weight = [rows_of(b) for b in triple_blocks]
-    out_weight = jnp.concatenate([rows_of(b) for b in out_blocks], axis=1)
-    up_weight = jnp.concatenate([rows_of(b) for b in up_blocks], axis=1)
-    down_weight = jnp.concatenate([rows_of(b) for b in down_blocks], axis=1)
+    hid_local = w_up.shape[1]
+    out_weight = jnp.concatenate([w[:, :head_block] for w in rest], axis=1)
+    up_weight = jnp.concatenate([w[:, head_block : head_block + hid_local] for w in rest], axis=1)
+    down_weight = jnp.concatenate([w[:, head_block + hid_local :] for w in rest], axis=1)
 
     triple = jnp.stack([dot(w, states, ((0,), (0,))) for w in triple_weight]) + triple_bias[:, :, None]
     triple = triple.reshape(cols, 3, head_local, head_width, tokens)
@@ -232,16 +231,16 @@
     grad2_low = grad2.astype(bf16)
 
     ff = up_weight.shape[1]
-    w_down_grad = weight_grad(grad2_low, hidden_low.reshape(cols, ff // cols, tokens), row_parts, share)
+    w_down_grad = finish_grad(partial_grad(grad2_low, hidden_low.reshape(cols, ff // cols, tokens), row_parts), share)
     b_down_grad = jnp.sum(grad2_low.astype(f32), axis=1)
     grad_up_low = (dot(down_weight, grad2_low, ((0,), (0,))) * slope).astype(bf16)
-    w_up_grad = weight_grad(normed_low, grad_up_low.reshape(cols, ff // cols, tokens), row_parts, share)
+    w_up_grad = finish_grad(partial_grad(normed_low, grad_up_low.reshape(cols, ff // cols, tokens), row_parts), share)
     b_up_grad = jnp.sum(grad_up_low.astype(f32), axis=1)
     grad_normed = grad2 + dot(up_weight, grad_up_low, ((1,), (0,)))
     grad1, gain1_grad, shift1_grad = norm_backward(grad_normed, normal1, scale1, gain1)
     grad1_low = grad1.astype(bf16)
 
-    w_out_grad = weight_grad(grad1_low, attended_low.reshape(cols, head_block, tokens), row_parts, share)
+    out_parts = partial_grad(grad1_low, attended_low.reshape(cols, head_block, tokens), row_parts)
     b_out_grad = jnp.sum(grad1_low.astype(f32), axis=1)
     grad_att = dot(out_weight, grad1_low, ((0,), (0,))).reshape(heads, head_width, tokens)
     grad_num = (grad_att * inverse[:, None, :]).astype(bf16)
@@ -264,13 +263,17 @@
     grad_feat_key = jnp.einsum("hdt,hdm->hmt", value_low, grad_kv_low, preferred_element_type=f32)
     grad_feat_key = grad_feat_key + grad_total[:, :, None]
     grad_key = feature_back(grad_feat_key, feat_key, key_scaled)
-    grad_value = jnp.einsum("hmt,hdm->hdt", key_low, grad_kv_low, preferred_element_type=f32) if False else jnp.einsum(
+    grad_value = jnp.einsum(
         "hdm,hmt->hdt", grad_kv_low, key_low, preferred_element_type=f32
     ).astype(bf16)
     grad_triple = jnp.stack(
         [g.reshape(cols, head_block, tokens) for g in (grad_query, grad_key, grad_value)], axis=1
     ).reshape(cols, 3 * head_block, tokens)
-    w_triple_grad = weight_grad(states, grad_triple, row_parts, share)
+    triple_parts = partial_grad(states, grad_triple, row_parts)
+    both = [jnp.concatenate((a, b), axis=3) for a, b in zip(triple_parts, out_parts)]
+    both = finish_grad(both, share)
+    w_triple_grad = both[:, : 3 * head_block]
+    w_out_grad = both[:, 3 * head_block :]
     b_triple_grad = jnp.sum(grad_triple.astype(f32), axis=2)
     grad_input = grad1
     for i in range(cols):
@@ -282,9 +285,8 @@
     ).reshape(6, row_parts, feat_local)
     row_small = jnp.transpose(row_small, (1, 0, 2)).reshape(row_parts, 6 * feat_local)
     col_small = jnp.concatenate((b_triple_grad, b_up_grad.reshape(cols, ff // cols)), axis=1)
-    got = row_small[0]
-    for j in (1, 2, 3):
-        got = got + swap(row_small[j], "row", j)
+    got = row_small[:2] + swap(row_small[2:], "row", 1)
+    got = got[0] + swap(got[1], "row", 2)
     got_col = col_small[0] + swap(col_small[1], "col", 1)
     got = got + swap(got, "col", 1)
     got_col = reduce_small(got_col, ("row",))

time: 499 us -> 480 us (0.962)
  starting transfers between devices: 120 us -> 64 us
  local copies, waits for them, and re-layouts: 53.7 us -> 77.1 us
  matrix products: 89.7 us -> 66.4 us
  other arithmetic: 58.8 us -> 80.1 us
  waiting for transfers between devices: 163 us -> 180 us
    ppermute x111 -> x55, starting transfers between devices: 120 us -> 49.4 us  [swap(): return lax.ppermute(value, axis, [(s, s ^ mask) for s in range(size)])]
    ppermute x0 -> x9, waiting for transfers between devices: none -> 57.1 us  [the longest x3 36.1 us: reduce_dp(): back = lax.ppermute(low, 'dp', [(1, 0), (2, 3)])]
    ppermute x111 -> x55, waiting for transfers between devices: 163 us -> 123 us  [swap(): return lax.ppermute(value, axis, [(s, s ^ mask) for s in range(size)])]
    concatenate x4 -> x18, other arithmetic: 1.76 us -> 29.8 us  [the longest x1 13.4 us: shards(): jnp.concatenate([w[:, head_block:head_block + hid_local] for w in rest],...]
    dot_general x26 -> x18, matrix products: 66.4 us -> 44.2 us  [dot(): return lax.dot_general(a, b, (dims, ((), ())), preferred_element_type=f32)]
    convert_element_type x2 -> x6, local copies, waits for them, and re-layouts: 4.66 us -> 23.3 us  [the longest x4 20.1 us: reduce_plane(): got = swap(theirs.astype(bf16), 'row', 1)]
    another operation x13 -> x6, local copies, waits for them, and re-layouts: 17.7 us -> 0.71 us  [the longest x8 17.3 us: reduce_plane(): got = swap(jnp.stack(theirs).astype(bf16), 'row', 1)]
    ppermute x0 -> x9, starting transfers between devices: none -> 14.6 us  [the longest x3 8.59 us: reduce_dp(): value = value + lax.ppermute(low, 'dp', [(0, 1), (3, 2)])]
  transfers between devices with their start and end apart: 111 -> 64, of which waited for: 38 -> 31; matrix products, arithmetic and copies ran while one was open for 30% -> 32% of each run, Pallas kernels for 0% -> 0%
where the time goes in v2:
time: 480 us; the launch traced here: 474 us
  waiting for transfers between devices  180 us (38%)
  other arithmetic  80.1 us (17%)
  local copies, waits for them, and re-layouts  77.1 us (16%)
  matrix products  66.4 us (14%)
  starting transfers between devices  64 us (13%)
  between operations  6.02 us (1%)
    ppermute x55, waiting for transfers between devices, swap(): return lax.ppermute(value, axis, [(s, s ^ mask) for s in range(size)])  123 us
    ppermute x55, starting transfers between devices, swap(): return lax.ppermute(value, axis, [(s, s ^ mask) for s in range(size)])  49.4 us
    dot_general x18, matrix products, dot(): return lax.dot_general(a, b, (dims, ((), ())), preferred_element_type=f32)  44.2 us
    ppermute x3, waiting for transfers between devices, reduce_dp(): back = lax.ppermute(low, 'dp', [(1, 0), (2, 3)])  36.1 us
    ppermute x3, waiting for transfers between devices, reduce_dp(): value = value + lax.ppermute(low, 'dp', [(0, 1), (3, 2)])  21 us
    convert_element_type x4, local copies, waits for them, and re-layouts, reduce_plane(): got = swap(theirs.astype(bf16), 'row', 1)  20.1 us
    unnamed x234, local copies, waits for them, and re-layouts  16.6 us
    reshape x2, local copies, waits for them, and re-layouts, partial_grad(): mine = dot(left[:2 * n], flat, ((1,), (1,))).reshape(2, n, cols, k)  14.4 us
  transfers between devices with their start and end apart: 64, of which 31 were waited for; matrix products, arithmetic and copies ran while one was open for 32% of the time, Pallas kernels for 0%

profile of v2, /device:TPU:0, one launch (start us, length us, event | category | flops | bytes accessed | tf_op | source)
XLA Modules:
  0.0 473.9 jit_solution(1146239394529939872)
XLA Ops:
  3.7 3.0 collective-permute-start.2
  24.0 12.2 %collective-permute-done.17 = f32[6,192]{1,0:T(8,128)S(1)} collective-permute-done((f32[6,192]{1,0:T(8,128)S(1)}, f32[6,192]{1,0:T(8,128)S(1)}, u32[]{:S(2)}, u32[]{:S(2)}) %collective-permute-start.17) | collective-permute-done | bytes 4640 | tf_op jit(solution)/shard_map/ppermute | solution.py:18
  36.2 2.8 collective-permute-start.22
  54.9 7.4 %collective-permute-done.8 = bf16[192,1152]{1,0:T(8,128)(2,1)S(1)} collective-permute-done((bf16[192,1152]{1,0:T(8,128)(2,1)}, bf16[192,1152]{1,0:T(8,128)(2,1)S(1)}, u32[]{:S(2)}, u32[]{:S(2)}) %collective-permute-start.8) | collective-permute-done | bytes 442400 | tf_op jit(solution)/shard_map/ppermute | solution.py:18
  64.0 6.7 %collective-permute-done.1 = bf16[384,512]{1,0:T(8,128)(2,1)S(1)} collective-permute-done((bf16[384,512]{1,0:T(8,128)(2,1)S(1)}, bf16[384,512]{1,0:T(8,128)(2,1)S(1)}, u32[]{:S(2)}, u32[]{:S(2)}) %collective-permute-start.1) | collective-permute-done | bytes 393248 | tf_op jit(solution)/shard_map/ppermute | solution.py:18
  72.1 6.6 %collective-permute-done.24 = bf16[384,512]{1,0:T(8,128)(2,1)S(1)} collective-permute-done((bf16[384,512]{1,0:T(8,128)(2,1)S(1)}, bf16[384,512]{1,0:T(8,128)(2,1)S(1)}, u32[]{:S(2)}, u32[]{:S(2)}) %collective-permute-start.24) | collective-permute-done | bytes 393248 | tf_op jit(solution)/shard_map/ppermute | solution.py:18
  79.5 2.5 collective-permute-done.11
  88.4 2.6 constant_dynamic-update-slice_fusion.3
  92.2 3.0 collective-permute-done.5
  101.5 3.2 fusion.24
  111.9 3.3 pad_maximum_fusion.6
  124.0 8.5 %collective-permute-done.16 = bf16[784,256]{1,0:T(8,128)(2,1)S(1)} collective-permute-done((bf16[784,256]{1,0:T(8,128)(2,1)S(1)}, bf16[784,256]{1,0:T(8,128)(2,1)S(1)}, u32[]{:S(2)}, u32[]{:S(2)}) %collective-permute-start.16) | collective-permute-done | bytes 401440 | tf_op jit(solution)/shard_map/ppermute | solution.py:18
  140.9 13.4 %fusion.12 = (bf16[768,3072]{1,0:T(8,128)(2,1)S(1)}, bf16[768,3072]{1,0:T(8,128)(2,1)}) fusion(bf16[384,3456]{1,0:T(8,128)(2,1)} %collective-permute-done.3, bf16[192,3456]{1,0:T(8,128)(2,1)S(1)} %collective-permute-done.2, bf16[192,1536]{1,0:T(8,128)(2,1)S(1)} %convert.87, bf16[192,1536]{1,0:T(8,128)(2,1)S(1)} %convert.86, ...), kind=kLoop, calls=%fused_computation.21 | loop fusion | flops 66060288 | bytes 19464192 | tf_op jit(solution)/shard_map/concatenate | solution.py:180
  154.4 5.2 %multiply_convert_fusion = (bf16[3072,512]{0,1:T(8,128)(2,1)S(1)}, f32[3072,512]{0,1:T(8,128)}) fusion(f32[3072]{0:T(1024)S(1)} %copy-done.89, bf16[768,3072]{1,0:T(8,128)(2,1)S(1)} %get-tuple-element.56, bf16[768,512]{1,0:T(8,128)(2,1)S(1)} %fusion.36), kind=kOutput, calls=%fused_computation.13 | convolution fusion | flops 2425356288 | bytes 14954496 | tf_op jit(solution)/shard_map/dot_general | solution.py:22
  159.6 2.7 fusion.108
  162.7 2.7 multiply_reduce_fusion.2
  166.7 7.9 %convert_reduce_fusion = (f32[3072]{0:T(1024)}, bf16[3072,512]{0,1:T(8,128)(2,1)S(1)}) fusion(f32[3072,512]{0,1:T(8,128)} %get-tuple-element.124, f32[3072]{0:T(1024)S(1)} %copy-done.90, bf16[768,3072]{1,0:T(8,128)(2,1)S(1)} %copy-done.14, bf16[768,512]{1,0:T(8,128)(2,1)S(1)} %get-tuple-element.43), kind=kOutput, calls=%fused_computation.10 | convolution fusion | flops 2436363264 | bytes 14966784 | tf_op jit(solution)/shard_map/dot_general | solution.py:22
  174.7 4.1 multiply_reduce_fusion.3
  182.9 3.5 fusion.67
  186.4 2.8 convolution_convert_fusion.1
  189.2 3.6 fusion.64
  192.8 2.8 convolution_convert_fusion
  201.0 4.1 fusion.124
  210.8 7.2 %reshape.258 = f32[2,192,2,1536]{3,2,1,0:T(2,128)} reshape(f32[384,3072]{1,0:T(8,128)} %fusion.67) | data formatting | bytes 9437184 | tf_op jit(solution)/shard_map/reshape | solution.py:135
  218.0 6.5 %convert_element_type.367 = bf16[2,192,2,1536]{3,2,1,0:T(2,128)(2,1)} reshape(bf16[384,3072]{1,0:T(8,128)(2,1)} %convolution_convert_fusion.1) | data formatting | bytes 4718592 | tf_op jit(solution)/shard_map/convert_element_type | solution.py:41
  224.5 3.5 copy.46
  236.1 3.4 fusion.27
  239.5 7.2 %reshape.259 = f32[2,192,2,1536]{3,2,1,0:T(2,128)} reshape(f32[384,3072]{1,0:T(8,128)} %fusion.64) | data formatting | bytes 9437184 | tf_op jit(solution)/shard_map/reshape | solution.py:135
  246.7 6.6 %convert_element_type.380 = bf16[2,192,2,1536]{3,2,1,0:T(2,128)(2,1)} reshape(bf16[384,3072]{1,0:T(8,128)(2,1)} %convolution_convert_fusion) | data formatting | bytes 4718592 | tf_op jit(solution)/shard_map/convert_element_type | solution.py:41
  253.3 3.5 copy.48
  263.5 9.6 %collective-permute-done.29 = bf16[784,256]{1,0:T(8,128)(2,1)S(1)} collective-permute-done((bf16[784,256]{1,0:T(8,128)(2,1)S(1)}, bf16[784,256]{1,0:T(8,128)(2,1)S(1)}, u32[]{:S(2)}, u32[]{:S(2)}) %collective-permute-start.29) | collective-permute-done | bytes 401440 | tf_op jit(solution)/shard_map/ppermute | solution.py:18
  294.1 6.0 %collective-permute-done.32 = f32[2688]{0:T(1024)S(1)} collective-permute-done((f32[2688]{0:T(1024)S(1)}, f32[2688]{0:T(1024)S(1)}, u32[]{:S(2)}, u32[]{:S(2)}) %collective-permute-start.32) | collective-permute-done | bytes 10784 | tf_op jit(solution)/shard_map/ppermute | solution.py:18
  303.9 2.6 collective-permute-start.37
  317.0 4.1 copy_add_fusion.1
  323.5 2.7 copy_add_fusion
  331.0 2.5 collective-permute-done.51
  337.4 3.5 collective-permute-done.49
  342.0 8.3 %collective-permute-done.57 = bf16[144,1536]{1,0:T(8,128)(2,1)S(1)} collective-permute-done((bf16[144,1536]{1,0:T(8,128)(2,1)S(1)}, bf16[144,1536]{1,0:T(8,128)(2,1)S(1)}, u32[]{:S(2)}, u32[]{:S(2)}) %collective-permute-start.57) | collective-permute-done | bytes 442400 | tf_op jit(solution)/shard_map/ppermute | solution.py:18
  355.6 15.1 %collective-permute-done.43 = bf16[48,1536]{1,0:T(8,128)(2,1)S(1)} collective-permute-done((bf16[48,1536]{1,0:T(8,128)(2,1)S(1)}, bf16[48,1536]{1,0:T(8,128)(2,1)S(1)}, u32[]{:S(2)}, u32[]{:S(2)}) %collective-permute-start.43) | collective-permute-done | bytes 147488 | tf_op jit(solution)/shard_map/ppermute | solution.py:18
  372.3 12.0 %collective-permute-done.41 = bf16[144,1536]{1,0:T(8,128)(2,1)S(1)} collective-permute-done((bf16[144,1536]{1,0:T(8,128)(2,1)S(1)}, bf16[144,1536]{1,0:T(8,128)(2,1)S(1)}, u32[]{:S(2)}, u32[]{:S(2)}) %collective-permute-start.41) | collective-permute-done | bytes 442400 | tf_op jit(solution)/shard_map/ppermute | solution.py:18
  386.8 3.5 collective-permute-start.53
  392.1 6.8 %collective-permute-done.44 = bf16[192,1536]{1,0:T(8,128)(2,1)S(1)} collective-permute-done((bf16[192,1536]{1,0:T(8,128)(2,1)S(1)}, bf16[192,1536]{1,0:T(8,128)(2,1)S(1)}, u32[]{:S(2)}, u32[]{:S(2)}) %collective-permute-start.44) | collective-permute-done | bytes 589856 | tf_op jit(solution)/shard_map/ppermute | solution.py:18
  400.6 3.5 collective-permute-start.45
  405.1 11.5 %collective-permute-done.61 = bf16[192,1536]{1,0:T(8,128)(2,1)S(1)} collective-permute-done((bf16[192,1536]{1,0:T(8,128)(2,1)S(1)}, bf16[192,1536]{1,0:T(8,128)(2,1)S(1)}, u32[]{:S(2)}, u32[]{:S(2)}) %collective-permute-start.61) | collective-permute-done | bytes 589856 | tf_op jit(solution)/shard_map/ppermute | solution.py:65
  417.6 9.5 %collective-permute-done.45 = bf16[192,1536]{1,0:T(8,128)(2,1)S(1)} collective-permute-done((bf16[192,1536]{1,0:T(8,128)(2,1)S(1)}, bf16[192,1536]{1,0:T(8,128)(2,1)S(1)}, u32[]{:S(2)}, u32[]{:S(2)}) %collective-permute-start.45) | collective-permute-done | bytes 589856 | tf_op jit(solution)/shard_map/ppermute | solution.py:65
  433.2 16.0 %collective-permute-done.55 = bf16[192,1536]{1,0:T(8,128)(2,1)S(1)} collective-permute-done((bf16[192,1536]{1,0:T(8,128)(2,1)S(1)}, bf16[192,1536]{1,0:T(8,128)(2,1)S(1)}, u32[]{:S(2)}, u32[]{:S(2)}) %collective-permute-start.55) | collective-permute-done | bytes 589856 | tf_op jit(solution)/shard_map/ppermute | solution.py:68
  450.2 11.5 %collective-permute-done.63 = bf16[192,1536]{1,0:T(8,128)(2,1)S(1)} collective-permute-done((bf16[192,1536]{1,0:T(8,128)(2,1)S(1)}, bf16[192,1536]{1,0:T(8,128)(2,1)S(1)}, u32[]{:S(2)}, u32[]{:S(2)}) %collective-permute-start.63) | collective-permute-done | bytes 589856 | tf_op jit(solution)/shard_map/ppermute | solution.py:68
  462.9 8.5 %collective-permute-done.47 = bf16[192,1536]{1,0:T(8,128)(2,1)S(1)} collective-permute-done((bf16[192,1536]{1,0:T(8,128)(2,1)S(1)}, bf16[192,1536]{1,0:T(8,128)(2,1)S(1)}, u32[]{:S(2)}, u32[]{:S(2)}) %collective-permute-start.47) | collective-permute-done | bytes 589856 | tf_op jit(solution)/shard_map/ppermute | solution.py:68
  (540 shorter events, 178.1 us)
Async XLA Ops:
  3.7 78.5 %collective-permute-start.2 = (bf16[192,3456]{1,0:T(8,128)(2,1)}, bf16[192,3456]{1,0:T(8,128)(2,1)S(1)}, u32[]{:S(2)}, u32[]{:S(2)}) collective-permute-start(bf16[192,3456]{1,0:T(8,128)(2,1)} %pad_maximum_fusion.10), channel_id=1, source_target_pairs={{0,4},{2,6},{4,0},{6,2},{1,5},{3,7},{5,1},{7,3},{8,12},{10,14},{12... | collective-permute-start | bytes 3981320 | tf_op jit(solution)/shard_map/ppermute | solution.py:18
  6.6 77.7 %collective-permute-start.4 = (bf16[192,3456]{1,0:T(8,128)(2,1)}, bf16[192,3456]{1,0:T(8,128)(2,1)}, u32[]{:S(2)}, u32[]{:S(2)}) collective-permute-start(bf16[192,3456]{1,0:T(8,128)(2,1)} %pad_maximum_fusion.10), channel_id=1, source_target_pairs={{0,1},{1,0},{2,3},{3,2},{4,5},{5,4},{6,7},{7,6},{8,9},{9,8},{10,11... | collective-permute-start | bytes 3981320 | tf_op jit(solution)/shard_map/ppermute | solution.py:18
  8.2 27.9 %collective-permute-start.17 = (f32[6,192]{1,0:T(8,128)S(1)}, f32[6,192]{1,0:T(8,128)S(1)}, u32[]{:S(2)}, u32[]{:S(2)}) collective-permute-start(f32[6,192]{1,0:T(8,128)S(1)} %stack.75), channel_id=1, source_target_pairs={{0,4},{2,6},{4,0},{6,2},{1,5},{3,7},{5,1},{7,3},{8,12},{10,14},{12... | collective-permute-start | bytes 13832 | tf_op jit(solution)/shard_map/ppermute | solution.py:18
  8.8 39.2 %collective-permute-start.14 = (bf16[6,64,256]{2,1,0:T(8,128)(2,1)}, bf16[6,64,256]{2,1,0:T(8,128)(2,1)}, u32[]{:S(2)}, u32[]{:S(2)}) collective-permute-start(bf16[6,64,256]{2,1,0:T(8,128)(2,1)} %param.23), channel_id=1, source_target_pairs={{0,1},{1,0},{2,3},{3,2},{4,5},{5,4},{6,7},{7,6},{8,9},{9,8},{10,11... | collective-permute-start | bytes 589832 | tf_op jit(solution)/shard_map/ppermute | solution.py:18
  10.2 13.8 %collective-permute-start.21 = (f32[8,128]{1,0:T(8,128)S(1)}, f32[8,128]{1,0:T(8,128)S(1)}, u32[]{:S(2)}, u32[]{:S(2)}) collective-permute-start(f32[8,128]{1,0:T(8,128)S(1)} %add.302), channel_id=1, source_target_pairs={{0,8},{8,0},{16,24},{24,16},{1,9},{9,1},{17,25},{25,17},{2,10},{10... | collective-permute-start | bytes 12296 | tf_op jit(solution)/shard_map/ppermute | solution.py:18
  23.9 25.1 %collective-permute-start = (bf16[384,512]{1,0:T(8,128)(2,1)}, bf16[384,512]{1,0:T(8,128)(2,1)}, u32[]{:S(2)}, u32[]{:S(2)}) collective-permute-start(bf16[384,512]{1,0:T(8,128)(2,1)} %pad_maximum_fusion.21), channel_id=1, source_target_pairs={{0,2},{2,0},{4,6},{6,4},{1,3},{3,1},{5,7},{7,5},{8,10},{10,8},{12,... | collective-permute-start | bytes 1179656 | tf_op jit(solution)/shard_map/ppermute | solution.py:18
  45.5 18.4 %collective-permute-start.10 = (bf16[192,1152]{1,0:T(8,128)(2,1)}, bf16[192,1152]{1,0:T(8,128)(2,1)S(1)}, u32[]{:S(2)}, u32[]{:S(2)}) collective-permute-start(bf16[192,1152]{1,0:T(8,128)(2,1)} %pad_maximum_fusion.20), channel_id=1, source_target_pairs={{0,1},{1,0},{2,3},{3,2},{4,5},{5,4},{6,7},{7,6},{8,9},{9,8},{10,11... | collective-permute-start | bytes 1327112 | tf_op jit(solution)/shard_map/ppermute | solution.py:18
  49.0 13.3 %collective-permute-start.8 = (bf16[192,1152]{1,0:T(8,128)(2,1)}, bf16[192,1152]{1,0:T(8,128)(2,1)S(1)}, u32[]{:S(2)}, u32[]{:S(2)}) collective-permute-start(bf16[192,1152]{1,0:T(8,128)(2,1)} %pad_maximum_fusion.20), channel_id=1, source_target_pairs={{0,4},{2,6},{4,0},{6,2},{1,5},{3,7},{5,1},{7,3},{8,12},{10,14},{12... | collective-permute-start | bytes 1327112 | tf_op jit(solution)/shard_map/ppermute | solution.py:18
  52.7 18.1 %collective-permute-start.1 = (bf16[384,512]{1,0:T(8,128)(2,1)S(1)}, bf16[384,512]{1,0:T(8,128)(2,1)S(1)}, u32[]{:S(2)}, u32[]{:S(2)}) collective-permute-start(bf16[384,512]{1,0:T(8,128)(2,1)S(1)} %pad_maximum_fusion.22), channel_id=1, source_target_pairs={{0,4},{2,6},{4,0},{6,2},{1,5},{3,7},{5,1},{7,3},{8,12},{10,14},{12... | collective-permute-start | bytes 1179656 | tf_op jit(solution)/shard_map/ppermute | solution.py:18
  62.3 16.4 %collective-permute-start.24 = (bf16[384,512]{1,0:T(8,128)(2,1)S(1)}, bf16[384,512]{1,0:T(8,128)(2,1)S(1)}, u32[]{:S(2)}, u32[]{:S(2)}) collective-permute-start(bf16[384,512]{1,0:T(8,128)(2,1)S(1)} %pad_maximum_fusion.26), channel_id=1, source_target_pairs={{0,4},{2,6},{4,0},{6,2},{1,5},{3,7},{5,1},{7,3},{8,12},{10,14},{12... | collective-permute-start | bytes 1179656 | tf_op jit(solution)/shard_map/ppermute | solution.py:18
  63.9 27.1 %collective-permute-start.9 = (bf16[384,1152]{1,0:T(8,128)(2,1)S(1)}, bf16[384,1152]{1,0:T(8,128)(2,1)S(1)}, u32[]{:S(2)}, u32[]{:S(2)}) collective-permute-start(bf16[384,1152]{1,0:T(8,128)(2,1)S(1)} %pad_maximum_fusion.11), channel_id=1, source_target_pairs={{0,2},{2,0},{4,6},{6,4},{1,3},{3,1},{5,7},{7,5},{8,10},{10,8},{12,... | collective-permute-start | bytes 2654216 | tf_op jit(solution)/shard_map/ppermute | solution.py:18
  70.8 11.2 %collective-permute-start.11 = (bf16[192,1152]{1,0:T(8,128)(2,1)S(1)}, bf16[192,1152]{1,0:T(8,128)(2,1)S(1)}, u32[]{:S(2)}, u32[]{:S(2)}) collective-permute-start(bf16[192,1152]{1,0:T(8,128)(2,1)S(1)} %collective-permute-done.8), channel_id=1, source_target_pairs={{0,1},{1,0},{2,3},{3,2},{4,5},{5,4},{6,7},{7,6},{8,9},{9,8},{10,11... | collective-permute-start | bytes 1327112 | tf_op jit(solution)/shard_map/ppermute | solution.py:18
  82.0 13.9 %collective-permute-start.12 = (bf16[384,1152]{1,0:T(8,128)(2,1)S(1)}, bf16[384,1152]{1,0:T(8,128)(2,1)S(1)}, u32[]{:S(2)}, u32[]{:S(2)}) collective-permute-start(bf16[384,1152]{1,0:T(8,128)(2,1)S(1)} %pad_maximum_fusion.12), channel_id=1, source_target_pairs={{0,2},{2,0},{4,6},{6,4},{1,3},{3,1},{5,7},{7,5},{8,10},{10,8},{12,... | collective-permute-start | bytes 2654216 | tf_op jit(solution)/shard_map/ppermute | solution.py:18
  83.8 54.2 %collective-permute-start.3 = (bf16[384,3456]{1,0:T(8,128)(2,1)}, bf16[384,3456]{1,0:T(8,128)(2,1)}, u32[]{:S(2)}, u32[]{:S(2)}) collective-permute-start(bf16[384,3456]{1,0:T(8,128)(2,1)} %pad_maximum_fusion.5), channel_id=1, source_target_pairs={{0,2},{2,0},{4,6},{6,4},{1,3},{3,1},{5,7},{7,5},{8,10},{10,8},{12,... | collective-permute-start | bytes 7962632 | tf_op jit(solution)/shard_map/ppermute | solution.py:18
  85.3 9.8 %collective-permute-start.5 = (bf16[48,3456]{1,0:T(8,128)(2,1)S(1)}, bf16[48,3456]{1,0:T(8,128)(2,1)S(1)}, u32[]{:S(2)}, u32[]{:S(2)}) collective-permute-start(bf16[48,3456]{1,0:T(8,128)(2,1)S(1)} %slice.570), channel_id=1, source_target_pairs={{0,4},{2,6},{4,0},{6,2},{1,5},{3,7},{5,1},{7,3},{8,12},{10,14},{12... | collective-permute-start | bytes 995336 | tf_op jit(solution)/shard_map/ppermute | solution.py:18
  87.9 24.0 %collective-permute-start.6 = (bf16[144,3456]{1,0:T(8,128)(2,1)}, bf16[144,3456]{1,0:T(8,128)(2,1)}, u32[]{:S(2)}, u32[]{:S(2)}) collective-permute-start(bf16[144,3456]{1,0:T(8,128)(2,1)} %slice.571), channel_id=1, source_target_pairs={{0,1},{1,0},{2,3},{3,2},{4,5},{5,4},{6,7},{7,6},{8,9},{9,8},{10,11... | collective-permute-start | bytes 2985992 | tf_op jit(solution)/shard_map/ppermute | solution.py:18
  115.2 19.5 %collective-permute-start.7 = (bf16[384,3456]{1,0:T(8,128)(2,1)}, bf16[384,3456]{1,0:T(8,128)(2,1)}, u32[]{:S(2)}, u32[]{:S(2)}) collective-permute-start(bf16[384,3456]{1,0:T(8,128)(2,1)} %pad_maximum_fusion.6), channel_id=1, source_target_pairs={{0,2},{2,0},{4,6},{6,4},{1,3},{3,1},{5,7},{7,5},{8,10},{10,8},{12,... | collective-permute-start | bytes 7962632 | tf_op jit(solution)/shard_map/ppermute | solution.py:18
  121.2 11.4 %collective-permute-start.16 = (bf16[784,256]{1,0:T(8,128)(2,1)S(1)}, bf16[784,256]{1,0:T(8,128)(2,1)S(1)}, u32[]{:S(2)}, u32[]{:S(2)}) collective-permute-start(bf16[784,256]{1,0:T(8,128)(2,1)S(1)} %fusion.76), channel_id=1, source_target_pairs={{0,4},{2,6},{4,0},{6,2},{1,5},{3,7},{5,1},{7,3},{8,12},{10,14},{12... | collective-permute-start | bytes 1204232 | tf_op jit(solution)/shard_map/ppermute | solution.py:18
  196.8 61.3 %collective-permute-start.19 = (bf16[384,512]{1,0:T(8,128)(2,1)}, bf16[384,512]{1,0:T(8,128)(2,1)}, u32[]{:S(2)}, u32[]{:S(2)}) collective-permute-start(bf16[384,512]{1,0:T(8,128)(2,1)} %pad_maximum_fusion.23), channel_id=1, source_target_pairs={{0,4},{2,6},{4,0},{6,2},{1,5},{3,7},{5,1},{7,3},{8,12},{10,14},{12... | collective-permute-start | bytes 1179656 | tf_op jit(solution)/shard_map/ppermute | solution.py:18
  198.0 30.5 %collective-permute-start.33 = (f32[128]{0:T(128)S(1)}, f32[128]{0:T(128)S(1)}, u32[]{:S(2)}, u32[]{:S(2)}) collective-permute-start(f32[128]{0:T(128)S(1)} %broadcast_in_dim.2), channel_id=1, source_target_pairs={{0,2},{2,0},{4,6},{6,4},{1,3},{3,1},{5,7},{7,5},{8,10},{10,8},{12,... | collective-permute-start | bytes 1544 | tf_op jit(solution)/shard_map/ppermute | solution.py:18
  205.7 24.9 %collective-permute-start.25 = (f32[2,1152]{1,0:T(2,128)S(1)}, f32[2,1152]{1,0:T(2,128)S(1)}, u32[]{:S(2)}, u32[]{:S(2)}) collective-permute-start(f32[2,1152]{1,0:T(2,128)S(1)} %slice.483), channel_id=1, source_target_pairs={{0,2},{2,0},{4,6},{6,4},{1,3},{3,1},{5,7},{7,5},{8,10},{10,8},{12,... | collective-permute-start | bytes 27656 | tf_op jit(solution)/shard_map/ppermute | solution.py:18
  210.7 50.0 %collective-permute-start.28 = (bf16[784,256]{1,0:T(8,128)(2,1)}, bf16[784,256]{1,0:T(8,128)(2,1)}, u32[]{:S(2)}, u32[]{:S(2)}) collective-permute-start(bf16[784,256]{1,0:T(8,128)(2,1)} %fusion.58), channel_id=1, source_target_pairs={{0,2},{2,0},{4,6},{6,4},{1,3},{3,1},{5,7},{7,5},{8,10},{10,8},{12,... | collective-permute-start | bytes 1204232 | tf_op jit(solution)/shard_map/ppermute | solution.py:18
  228.0 89.0 %collective-permute-start.48 = (bf16[2,192,2,1536]{3,1,2,0:T(8,128)(2,1)}, bf16[2,192,2,1536]{3,1,2,0:T(8,128)(2,1)}, u32[]{:S(2)}, u32[]{:S(2)}) collective-permute-start(bf16[2,192,2,1536]{3,1,2,0:T(8,128)(2,1)} %copy.46), channel_id=1, source_target_pairs={{0,2},{2,0},{4,6},{6,4},{1,3},{3,1},{5,7},{7,5},{8,10},{10,8},{12,... | collective-permute-start | bytes 7077896 | tf_op jit(solution)/shard_map/ppermute | solution.py:18
  233.4 23.4 %collective-permute-start.35 = (f32[128]{0:T(128)S(1)}, f32[128]{0:T(128)}, u32[]{:S(2)}, u32[]{:S(2)}) collective-permute-start(f32[128]{0:T(128)S(1)} %fusion.173), channel_id=1, source_target_pairs={{0,1},{1,0},{2,3},{3,2},{4,5},{5,4},{6,7},{7,6},{8,9},{9,8},{10,11... | collective-permute-start | bytes 1544 | tf_op jit(solution)/shard_map/ppermute | solution.py:18
  235.0 22.4 %collective-permute-start.27 = (f32[1152]{0:T(1024)}, f32[1152]{0:T(1024)}, u32[]{:S(2)}, u32[]{:S(2)}) collective-permute-start(f32[1152]{0:T(1024)} %add.308), channel_id=1, source_target_pairs={{0,1},{1,0},{2,3},{3,2},{4,5},{5,4},{6,7},{7,6},{8,9},{9,8},{10,11... | collective-permute-start | bytes 13832 | tf_op jit(solution)/shard_map/ppermute | solution.py:18
  256.8 64.8 %collective-permute-start.56 = (bf16[2,192,2,1536]{3,1,2,0:T(8,128)(2,1)}, bf16[2,192,2,1536]{3,1,2,0:T(8,128)(2,1)}, u32[]{:S(2)}, u32[]{:S(2)}) collective-permute-start(bf16[2,192,2,1536]{3,1,2,0:T(8,128)(2,1)} %copy.48), channel_id=1, source_target_pairs={{0,2},{2,0},{4,6},{6,4},{1,3},{3,1},{5,7},{7,5},{8,10},{10,8},{12,... | collective-permute-start | bytes 7077896 | tf_op jit(solution)/shard_map/ppermute | solution.py:18
  261.8 11.3 %collective-permute-start.29 = (bf16[784,256]{1,0:T(8,128)(2,1)S(1)}, bf16[784,256]{1,0:T(8,128)(2,1)S(1)}, u32[]{:S(2)}, u32[]{:S(2)}) collective-permute-start(bf16[784,256]{1,0:T(8,128)(2,1)S(1)} %fusion.77), channel_id=1, source_target_pairs={{0,4},{2,6},{4,0},{6,2},{1,5},{3,7},{5,1},{7,3},{8,12},{10,14},{12... | collective-permute-start | bytes 1204232 | tf_op jit(solution)/shard_map/ppermute | solution.py:18
  281.4 9.4 %collective-permute-start.30 = (f32[2688]{0:T(1024)S(1)}, f32[2688]{0:T(1024)S(1)}, u32[]{:S(2)}, u32[]{:S(2)}) collective-permute-start(f32[2688]{0:T(1024)S(1)} %get-tuple-element.36), channel_id=1, source_target_pairs={{0,1},{1,0},{2,3},{3,2},{4,5},{5,4},{6,7},{7,6},{8,9},{9,8},{10,11... | collective-permute-start | bytes 32264 | tf_op jit(solution)/shard_map/ppermute | solution.py:18
  289.7 21.4 %collective-permute-start.38 = (bf16[384,512]{1,0:T(8,128)(2,1)}, bf16[384,512]{1,0:T(8,128)(2,1)}, u32[]{:S(2)}, u32[]{:S(2)}) collective-permute-start(bf16[384,512]{1,0:T(8,128)(2,1)} %pad_maximum_fusion.27), channel_id=1, source_target_pairs={{0,4},{2,6},{4,0},{6,2},{1,5},{3,7},{5,1},{7,3},{8,12},{10,14},{12... | collective-permute-start | bytes 1179656 | tf_op jit(solution)/shard_map/ppermute | solution.py:18
  303.4 48.1 %collective-permute-start.40 = (bf16[2,192,2,1536]{3,1,2,0:T(8,128)(2,1)}, bf16[2,192,2,1536]{3,1,2,0:T(8,128)(2,1)}, u32[]{:S(2)}, u32[]{:S(2)}) collective-permute-start(bf16[2,192,2,1536]{3,1,2,0:T(8,128)(2,1)} %pad_maximum_fusion.8), channel_id=1, source_target_pairs={{0,2},{2,0},{4,6},{6,4},{1,3},{3,1},{5,7},{7,5},{8,10},{10,8},{12,... | collective-permute-start | bytes 7077896 | tf_op jit(solution)/shard_map/ppermute | solution.py:18
  327.8 13.0 %collective-permute-start.49 = (bf16[144,1536]{1,0:T(8,128)(2,1)S(1)}, bf16[144,1536]{1,0:T(8,128)(2,1)S(1)}, u32[]{:S(2)}, u32[]{:S(2)}) collective-permute-start(bf16[144,1536]{1,0:T(8,128)(2,1)S(1)} %slice_bitcast_fusion.13), channel_id=1, source_target_pairs={{0,1},{1,0},{2,3},{3,2},{4,5},{5,4},{6,7},{7,6},{8,9},{9,8},{10,11... | collective-permute-start | bytes 1327112 | tf_op jit(solution)/shard_map/ppermute | solution.py:18
  330.0 20.3 %collective-permute-start.57 = (bf16[144,1536]{1,0:T(8,128)(2,1)S(1)}, bf16[144,1536]{1,0:T(8,128)(2,1)S(1)}, u32[]{:S(2)}, u32[]{:S(2)}) collective-permute-start(bf16[144,1536]{1,0:T(8,128)(2,1)S(1)} %slice_bitcast_fusion.12), channel_id=1, source_target_pairs={{0,1},{1,0},{2,3},{3,2},{4,5},{5,4},{6,7},{7,6},{8,9},{9,8},{10,11... | collective-permute-start | bytes 1327112 | tf_op jit(solution)/shard_map/ppermute | solution.py:18
  333.6 52.4 %collective-permute-start.52 = (bf16[192,1536]{1,0:T(8,128)(2,1)S(1)}, bf16[192,1536]{1,0:T(8,128)(2,1)S(1)}, u32[]{:S(2)}, u32[]{:S(2)}) collective-permute-start(bf16[192,1536]{1,0:T(8,128)(2,1)S(1)} %pad_maximum_fusion.17), channel_id=1, source_target_pairs={{0,1},{1,0},{2,3},{3,2},{4,5},{5,4},{6,7},{7,6},{8,9},{9,8},{10,11... | collective-permute-start | bytes 1769480 | tf_op jit(solution)/shard_map/ppermute | solution.py:18
  336.2 54.1 %collective-permute-start.60 = (bf16[192,1536]{1,0:T(8,128)(2,1)S(1)}, bf16[192,1536]{1,0:T(8,128)(2,1)S(1)}, u32[]{:S(2)}, u32[]{:S(2)}) collective-permute-start(bf16[192,1536]{1,0:T(8,128)(2,1)S(1)} %pad_maximum_fusion.19), channel_id=1, source_target_pairs={{0,1},{1,0},{2,3},{3,2},{4,5},{5,4},{6,7},{7,6},{8,9},{9,8},{10,11... | collective-permute-start | bytes 1769480 | tf_op jit(solution)/shard_map/ppermute | solution.py:18
  341.0 45.6 %collective-permute-start.50 = (bf16[192,1536]{1,0:T(8,128)(2,1)S(1)}, bf16[192,1536]{1,0:T(8,128)(2,1)S(1)}, u32[]{:S(2)}, u32[]{:S(2)}) collective-permute-start(bf16[192,1536]{1,0:T(8,128)(2,1)S(1)} %pad_maximum_fusion.16), channel_id=1, source_target_pairs={{0,4},{2,6},{4,0},{6,2},{1,5},{3,7},{5,1},{7,3},{8,12},{10,14},{12... | collective-permute-start | bytes 1769480 | tf_op jit(solution)/shard_map/ppermute | solution.py:18
  350.5 39.9 %collective-permute-start.58 = (bf16[192,1536]{1,0:T(8,128)(2,1)S(1)}, bf16[192,1536]{1,0:T(8,128)(2,1)S(1)}, u32[]{:S(2)}, u32[]{:S(2)}) collective-permute-start(bf16[192,1536]{1,0:T(8,128)(2,1)S(1)} %pad_maximum_fusion.18), channel_id=1, source_target_pairs={{0,4},{2,6},{4,0},{6,2},{1,5},{3,7},{5,1},{7,3},{8,12},{10,14},{12... | collective-permute-start | bytes 1769480 | tf_op jit(solution)/shard_map/ppermute | solution.py:18
  354.4 16.2 %collective-permute-start.43 = (bf16[48,1536]{1,0:T(8,128)(2,1)S(1)}, bf16[48,1536]{1,0:T(8,128)(2,1)S(1)}, u32[]{:S(2)}, u32[]{:S(2)}) collective-permute-start(bf16[48,1536]{1,0:T(8,128)(2,1)S(1)} %get-tuple-element.87), channel_id=1, source_target_pairs={{0,4},{2,6},{4,0},{6,2},{1,5},{3,7},{5,1},{7,3},{8,12},{10,14},{12... | collective-permute-start | bytes 442376 | tf_op jit(solution)/shard_map/ppermute | solution.py:18
  370.7 13.6 %collective-permute-start.41 = (bf16[144,1536]{1,0:T(8,128)(2,1)S(1)}, bf16[144,1536]{1,0:T(8,128)(2,1)S(1)}, u32[]{:S(2)}, u32[]{:S(2)}) collective-permute-start(bf16[144,1536]{1,0:T(8,128)(2,1)S(1)} %slice_bitcast_fusion.14), channel_id=1, source_target_pairs={{0,1},{1,0},{2,3},{3,2},{4,5},{5,4},{6,7},{7,6},{8,9},{9,8},{10,11... | collective-permute-start | bytes 1327112 | tf_op jit(solution)/shard_map/ppermute | solution.py:18
  384.3 14.6 %collective-permute-start.44 = (bf16[192,1536]{1,0:T(8,128)(2,1)S(1)}, bf16[192,1536]{1,0:T(8,128)(2,1)S(1)}, u32[]{:S(2)}, u32[]{:S(2)}) collective-permute-start(bf16[192,1536]{1,0:T(8,128)(2,1)S(1)} %pad_maximum_fusion.15), channel_id=1, source_target_pairs={{0,1},{1,0},{2,3},{3,2},{4,5},{5,4},{6,7},{7,6},{8,9},{9,8},{10,11... | collective-permute-start | bytes 1769480 | tf_op jit(solution)/shard_map/ppermute | solution.py:18
  386.0 14.4 %collective-permute-start.42 = (bf16[192,1536]{1,0:T(8,128)(2,1)S(1)}, bf16[192,1536]{1,0:T(8,128)(2,1)S(1)}, u32[]{:S(2)}, u32[]{:S(2)}) collective-permute-start(bf16[192,1536]{1,0:T(8,128)(2,1)S(1)} %pad_maximum_fusion.14), channel_id=1, source_target_pairs={{0,4},{2,6},{4,0},{6,2},{1,5},{3,7},{5,1},{7,3},{8,12},{10,14},{12... | collective-permute-start | bytes 1769480 | tf_op jit(solution)/shard_map/ppermute | solution.py:18
  386.8 17.3 %collective-permute-start.53 = (bf16[192,1536]{1,0:T(8,128)(2,1)S(1)}, bf16[192,1536]{1,0:T(8,128)(2,1)S(1)}, u32[]{:S(2)}, u32[]{:S(2)}) collective-permute-start(bf16[192,1536]{1,0:T(8,128)(2,1)S(1)} %fusion.101), channel_id=1, source_target_pairs={{0,8},{24,16},{1,9},{25,17},{2,10},{26,18},{3,11},{27,19},{4,12},{... | collective-permute-start | bytes 1769480 | tf_op jit(solution)/shard_map/ppermute | solution.py:65
  390.5 26.1 %collective-permute-start.61 = (bf16[192,1536]{1,0:T(8,128)(2,1)S(1)}, bf16[192,1536]{1,0:T(8,128)(2,1)S(1)}, u32[]{:S(2)}, u32[]{:S(2)}) collective-permute-start(bf16[192,1536]{1,0:T(8,128)(2,1)S(1)} %fusion.102), channel_id=1, source_target_pairs={{0,8},{24,16},{1,9},{25,17},{2,10},{26,18},{3,11},{27,19},{4,12},{... | collective-permute-start | bytes 1769480 | tf_op jit(solution)/shard_map/ppermute | solution.py:65
  400.6 26.5 %collective-permute-start.45 = (bf16[192,1536]{1,0:T(8,128)(2,1)S(1)}, bf16[192,1536]{1,0:T(8,128)(2,1)S(1)}, u32[]{:S(2)}, u32[]{:S(2)}) collective-permute-start(bf16[192,1536]{1,0:T(8,128)(2,1)S(1)} %fusion.100), channel_id=1, source_target_pairs={{0,8},{24,16},{1,9},{25,17},{2,10},{26,18},{3,11},{27,19},{4,12},{... | collective-permute-start | bytes 1769480 | tf_op jit(solution)/shard_map/ppermute | solution.py:65
  404.4 23.7 %collective-permute-start.54 = (bf16[192,1536]{1,0:T(8,128)(2,1)S(1)}, bf16[192,1536]{1,0:T(8,128)(2,1)S(1)}, u32[]{:S(2)}, u32[]{:S(2)}) collective-permute-start(bf16[192,1536]{1,0:T(8,128)(2,1)S(1)} %fusion.56), channel_id=1, source_target_pairs={{8,16},{16,8},{9,17},{17,9},{10,18},{18,10},{11,19},{19,11},{12,20... | collective-permute-start | bytes 1769480 | tf_op jit(solution)/shard_map/ppermute | solution.py:66
  416.9 12.9 %collective-permute-start.62 = (bf16[192,1536]{1,0:T(8,128)(2,1)S(1)}, bf16[192,1536]{1,0:T(8,128)(2,1)S(1)}, u32[]{:S(2)}, u32[]{:S(2)}) collective-permute-start(bf16[192,1536]{1,0:T(8,128)(2,1)S(1)} %fusion.57), channel_id=1, source_target_pairs={{8,16},{16,8},{9,17},{17,9},{10,18},{18,10},{11,19},{19,11},{12,20... | collective-permute-start | bytes 1769480 | tf_op jit(solution)/shard_map/ppermute | solution.py:66
  428.5 20.7 %collective-permute-start.55 = (bf16[192,1536]{1,0:T(8,128)(2,1)S(1)}, bf16[192,1536]{1,0:T(8,128)(2,1)S(1)}, u32[]{:S(2)}, u32[]{:S(2)}) collective-permute-start(bf16[192,1536]{1,0:T(8,128)(2,1)S(1)} %add_convert_fusion.1), channel_id=1, source_target_pairs={{8,0},{16,24},{9,1},{17,25},{10,2},{18,26},{11,3},{19,27},{12,4},{... | collective-permute-start | bytes 1769480 | tf_op jit(solution)/shard_map/ppermute | solution.py:68
  430.2 31.6 %collective-permute-start.63 = (bf16[192,1536]{1,0:T(8,128)(2,1)S(1)}, bf16[192,1536]{1,0:T(8,128)(2,1)S(1)}, u32[]{:S(2)}, u32[]{:S(2)}) collective-permute-start(bf16[192,1536]{1,0:T(8,128)(2,1)S(1)} %add_convert_fusion), channel_id=1, source_target_pairs={{8,0},{16,24},{9,1},{17,25},{10,2},{18,26},{11,3},{19,27},{12,4},{... | collective-permute-start | bytes 1769480 | tf_op jit(solution)/shard_map/ppermute | solution.py:68
  431.9 39.6 %collective-permute-start.47 = (bf16[192,1536]{1,0:T(8,128)(2,1)S(1)}, bf16[192,1536]{1,0:T(8,128)(2,1)S(1)}, u32[]{:S(2)}, u32[]{:S(2)}) collective-permute-start(bf16[192,1536]{1,0:T(8,128)(2,1)S(1)} %add_convert_fusion.2), channel_id=1, source_target_pairs={{8,0},{16,24},{9,1},{17,25},{10,2},{18,26},{11,3},{19,27},{12,4},{... | collective-permute-start | bytes 1769480 | tf_op jit(solution)/shard_map/ppermute | solution.py:68
  (130 other events, 953.2 us)
